TPU v7x, 32 devices: a whole 2x2x4 slice. The times are simulated.
32 devices in a mesh: rep: 4 (over y, x), fsdp: 8 (over z, core).
Axes of the slice: x: 2, y: 2, z: 4, core: 2. Of those that a mesh axis runs over, the one named last changes fastest.
Arguments:
- tokens: bfloat16 [6144, 4096], P(('rep', 'fsdp')), may hold values from -6 to 6
- cotangent: bfloat16 [6144, 256], P(('rep', 'fsdp')), may hold values from -6 to 6
- weight: float32 [4096, 256], P('fsdp'), may hold values from -0.09375 to 0.09375
- momentum: float32 [4, 4096, 256], P('rep', 'fsdp'), may hold values from -6 to 6
- column_order: int32 [64], replicated, may hold values from 0 to 63, each once
Outputs:
- input_grad: bfloat16 [6144, 4096], P(('rep', 'fsdp'))
- new_momentum: float32 [4, 4096, 256], P('rep', 'fsdp')
- update: float32 [4096, 256], P('fsdp')
- new_weight: float32 [4096, 256], P('fsdp')
Inputs may be any that keep to these rules, and one draw needn't show every extreme that they name: `column_order`: each of the 64 frequency indices appears exactly once.
All inputs are finite; a program needn't handle non-finite values.
Results may differ from a plain program's by a relative error of at most 0.0049.
Values may be sent and summed in bfloat16 or wider, within the bound.
No kernel may reach another device: no remote copies, remote signals or barrier semaphores. Data moves between devices by JAX's collectives and lax.ppermute only.
A program may use at most 64 MiB of HBM per device.

v0:
```python
import math

import jax
import jax.numpy as jnp
from jax import lax
from jax.sharding import PartitionSpec as P

KW = 256
BLOCK = 64
SEL = 16


MOMENTUM_DECAY = 0.9
LEARN_RATE = 0.05


def dct_table():
    index = jnp.arange(BLOCK).astype(jnp.float32)
    table = jnp.cos(
        math.pi * (2.0 * index[None, :] + 1.0) * index[:, None] / (2.0 * BLOCK)
    ) * math.sqrt(2.0 / BLOCK)
    return jnp.where(index[:, None] == 0.0, table * math.sqrt(0.5), table)


def on_device(tokens, cotangent, weight, momentum, column_order):
    members = lax.axis_size("fsdp")
    replicas = lax.axis_size("rep")
    rows_own = weight.shape[0]
    table = dct_table()
    weight_half = weight.astype(jnp.bfloat16)
    input_grad = lax.dot_general(
        cotangent,
        lax.all_gather(weight_half, "fsdp", axis=0, tiled=True),
        (((1,), (1,)), ((), ())),
        preferred_element_type=jnp.float32,
    ).astype(jnp.bfloat16)
    scale = float(tokens.shape[0] * members) ** (-0.5)
    weight_grad = (
        lax.psum_scatter(
            lax.dot_general(
                tokens, cotangent, (((0,), (0,)), ((), ())), preferred_element_type=jnp.float32
            ),
            "fsdp",
            scatter_dimension=0,
            tiled=True,
        )
        * scale
    )
    moment = MOMENTUM_DECAY * momentum[0] + weight_grad
    blocks = moment.reshape(rows_own // BLOCK, BLOCK, KW // BLOCK, BLOCK)
    coeffs = jnp.einsum("kn,anbm,lm->akbl", table, blocks, table, precision=lax.Precision.HIGHEST)
    picker = (jnp.arange(BLOCK)[:, None] == column_order[None, :SEL]).astype(jnp.float32)
    compact = jnp.einsum("akbl,ls->akbs", coeffs, picker, precision=lax.Precision.HIGHEST)
    sent = jnp.einsum("akbs,ls->akbl", compact, picker, precision=lax.Precision.HIGHEST)
    own_back = jnp.einsum("kn,akbl,lm->anbm", table, sent, table, precision=lax.Precision.HIGHEST)
    new_momentum = (moment - own_back.reshape(rows_own, KW))[None]
    flat_sent = compact.reshape(-1)
    gathered = lax.all_gather(flat_sent, "rep", axis=0, tiled=True)
    summed = jnp.sum(gathered.reshape(replicas, -1), axis=0)
    summed_full = jnp.einsum(
        "akbs,ls->akbl", summed.reshape(compact.shape), picker, precision=lax.Precision.HIGHEST
    )
    decoded = jnp.einsum(
        "kn,akbl,lm->anbm", table, summed_full, table, precision=lax.Precision.HIGHEST
    )
    update = decoded.reshape(rows_own, KW) / replicas
    new_weight = weight - LEARN_RATE * update
    return (input_grad, new_momentum, update, new_weight)


def solution(mesh):
    in_specs = (
        P(("rep", "fsdp"), None),
        P(("rep", "fsdp"), None),
        P("fsdp", None),
        P("rep", "fsdp", None),
        P(),
    )
    out_specs = (P(("rep", "fsdp"), None), P("rep", "fsdp", None), P("fsdp", None), P("fsdp", None))
    return jax.shard_map(
        on_device, mesh=mesh, in_specs=in_specs, out_specs=out_specs, check_vma=False
    )
```

profile of v0, /device:TPU:0, one launch (start us, length us, event | category | flops | bytes accessed | tf_op | source)
XLA Modules:
  0.0 147.0 jit_solution(15613769380523077113)
XLA Ops:
  7.2 0.0 copy-start
  7.2 0.0 all-gather.2.cloned.1.call-start
  7.2 1.9 %convert_element_type.31 = bf16[512,256]{1,0:T(8,128)(2,1)} convert(f32[512,256]{1,0:T(8,128)} %param.7) | non-fusion elementwise | flops 131072 | bytes 786432 | tf_op jit(solution)/shard_map/convert_element_type | solution.py:30
  9.1 0.0 all-gather.2.cloned.1.call-update
  9.1 0.0 reduce-scatter.2.cloned.1.call-start
  9.2 0.0 copy-done
  9.2 3.6 %fusion.78 = f32[4096,256]{1,0:T(8,128)} fusion(bf16[192,4096]{1,0:T(8,128)(2,1)S(1)} %copy-done, bf16[192,256]{1,0:T(8,128)(2,1)} %param.6), kind=kOutput, calls=%fused_computation.85 | convolution fusion | flops 402653184 | bytes 5865472 | tf_op jit(solution)/shard_map/dot_general | solution.py:40
  12.8 0.0 copy-start.2
  12.8 0.0 copy-start.4
  12.8 0.0 reduce-scatter.2.cloned.1.call-update
  12.8 1.0 copy-done.2
  13.8 1.0 copy.42
  14.8 0.0 copy-start.3
  14.9 27.2 %all-gather.2.cloned.1.call-done = bf16[4096,256]{1,0:T(8,128)(2,1)} async-done(((bf16[512,256]{1,0:T(8,128)(2,1)}), bf16[4096,256]{1,0:T(8,128)(2,1)}) %all-gather.2.cloned.1.call-update) | async-done | bytes 2097168 | tf_op jit(solution)/shard_map/all_gather | solution.py:33
  42.1 0.0 copy-done.4
  42.1 3.6 %convolution_convert_fusion = bf16[192,4096]{1,0:T(8,128)(2,1)} fusion(bf16[192,256]{1,0:T(8,128)(2,1)S(1)} %copy-done.4, bf16[4096,256]{1,0:T(8,128)(2,1)} %all-gather.2.cloned.1.call-done), kind=kOutput, calls=%fused_computation | convolution fusion | flops 403439616 | bytes 3768320 | tf_op jit(solution)/shard_map/dot_general | solution.py:31
  45.6 48.1 %reduce-scatter.2.cloned.1.call-done = f32[512,256]{1,0:T(8,128)} async-done(((f32[4096,256]{1,0:T(8,128)}), f32[512,256]{1,0:T(8,128)}) %reduce-scatter.2.cloned.1.call-update) | async-done | bytes 524304 | tf_op jit(solution)/shard_map/reduce_scatter | solution.py:39
  93.7 0.0 copy-done.3
  93.7 1.1 bitcast_add_fusion
  94.8 0.5 reshape.49
  95.3 0.0 copy-start.5
  95.3 1.3 fusion.2
  96.6 1.1 convolution_bitcast_fusion.1
  97.8 0.0 copy-done.5
  97.8 1.3 fusion.53
  99.1 0.4 copy.36
  99.5 1.7 %fusion.51 = f32[8,64,4,64]{1,3,2,0:T(8,128)} fusion(f32[8,64,4,16]{1,3,2,0:T(8,128)S(1)} %fusion.53, s32[16]{0:T(128)S(1)} %bitcast.53), kind=kOutput, calls=%fused_computation.59 | convolution fusion | flops 25166848 | bytes 655424 | tf_op jit(solution)/shard_map/akbs,ls->akbl/dot_general | solution.py:54
  101.2 0.7 reshape.51
  101.8 10.9 %all_gather.7 = f32[131072]{0:T(1024)S(1)} all-gather(f32[32768]{0:T(1024)S(1)} %reshape.51), channel_id=1, replica_groups=mesh['rep'=4,'fsdp'=8] {'rep'}, dimensions={0}, use_global_device_ids=true | all-gather | bytes 655360 | tf_op jit(solution)/shard_map/all_gather | solution.py:58
  112.7 0.2 reshape.52
  113.0 0.3 reduce_sum.9
  113.3 0.7 reshape.53
  114.0 1.7 %fusion = f32[8,64,4,64]{1,3,2,0:T(8,128)S(1)} fusion(f32[8,64,4,16]{3,2,1,0:T(4,128)S(1)} %reshape.53, s32[16]{0:T(128)S(1)} %bitcast.54), kind=kOutput, calls=%fused_computation.3 | convolution fusion | flops 25166848 | bytes 655424 | tf_op jit(solution)/shard_map/akbs,ls->akbl/dot_general | solution.py:60
  115.7 3.3 %fusion.6 = f32[8,4,64,64]{2,3,1,0:T(8,128)S(1)} fusion(f32[8,64,4,64]{1,3,2,0:T(8,128)S(1)} %fusion, f32[64]{0:T(128)S(1)} %iota_convert_fusion, f32[64]{0:T(128)S(1)} %add_multiply_fusion, pred[64]{0:T(512)(128)(4,1)S(1)} %broadcast_compare_fusion), kind=kOutput, calls=%fused_computation.13 | convolution fusion | flops 100683776 | bytes 1049152 | tf_op jit(solution)/shard_map/kn,akbl,lm->anbm/dot_general | solution.py:63
  119.0 2.2 %multiply_bitcast_fusion = (f32[8,64,4,64]{3,1,2,0:T(8,128)S(1)}, f32[8,64,4,64]{3,1,2,0:T(8,128)}) fusion(f32[8,4,64,64]{2,3,1,0:T(8,128)S(1)} %fusion.6, f32[64]{0:T(128)S(1)} %iota_convert_fusion, f32[64]{0:T(128)S(1)} %add_multiply_fusion, pred[64]{0:T(512)(128)(4,1)S(1)} %broadcast_compare_fusion), kind=kOutput, calls=%fused_computation.7 | convolution fusion | flops 100945920 | bytes 1573440 | tf_op jit(solution)/shard_map/kn,akbl,lm->anbm/dot_general | solution.py:63
  121.2 1.3 copy.41
  122.5 1.5 %mul.163 = f32[512,256]{0,1:T(8,128)S(1)} reshape(f32[8,64,4,64]{1,0,3,2:T(8,128)} %copy.41) | data formatting | bytes 1048576 | tf_op jit(solution)/shard_map/mul | solution.py:67
  124.0 1.1 sub.7
  125.1 1.0 copy.44
  126.1 0.0 copy-start.1
  126.1 3.0 %copy.52 = f32[8,64,4,64]{3,2,1,0:T(4,128)} copy(f32[8,64,4,64]{3,1,2,0:T(8,128)} %get-tuple-element.17) | data formatting | bytes 1048576
  129.1 2.6 %reshape.56 = f32[512,256]{1,0:T(8,128)} reshape(f32[8,64,4,64]{3,2,1,0:T(4,128)} %copy.52) | data formatting | bytes 1048576
  131.7 0.0 copy-done.1
  131.7 3.3 %fusion.9 = f32[8,4,64,64]{2,3,1,0:T(8,128)S(1)} fusion(f32[8,64,4,64]{1,3,2,0:T(8,128)S(1)} %copy-done.1, f32[64]{0:T(128)S(1)} %iota_convert_fusion, f32[64]{0:T(128)S(1)} %add_multiply_fusion, pred[64]{0:T(512)(128)(4,1)S(1)} %broadcast_compare_fusion), kind=kOutput, calls=%fused_computation.16 | convolution fusion | flops 100683776 | bytes 1049152 | tf_op jit(solution)/shard_map/kn,akbl,lm->anbm/dot_general | solution.py:55
  135.0 1.1 convolution_bitcast_fusion
  136.2 0.7 copy.35
  136.9 1.4 reshape.50
  138.3 1.9 %subtract_bitcast_fusion = f32[1,512,256]{2,1,0:T(8,128)} fusion(f32[512,256]{1,0:T(8,128)S(1)} %bitcast_add_fusion, f32[512,256]{1,0:T(8,128)} %reshape.50), kind=kLoop, calls=%fused_computation.10 | loop fusion | flops 131072 | bytes 1572864 | tf_op jit(solution)/shard_map/broadcast_in_dim | solution.py:56
  (3 shorter events, 0.0 us)
Async XLA Ops:
  7.2 2.0 %copy-start = (bf16[192,4096]{1,0:T(8,128)(2,1)S(1)}, bf16[192,4096]{1,0:T(8,128)(2,1)}, u32[]{:S(2)}) copy-start(bf16[192,4096]{1,0:T(8,128)(2,1)} %param.5) | copy-start | bytes 4718596
  7.2 34.9 %all-gather.2.cloned.1.call-start = ((), (), s32[]{:S(2)}) async-start(), calls=%async_computation.1 | async-start | bytes 2359296 | tf_op jit(solution)/shard_map/all_gather | solution.py:33
  9.1 84.6 %reduce-scatter.2.cloned.1.call-start = ((), (), s32[]{:S(2)}) async-start(), calls=%async_computation.2 | async-start | bytes 4718592 | tf_op jit(solution)/shard_map/reduce_scatter | solution.py:39
  12.8 1.0 copy-start.2
  12.8 29.3 %copy-start.4 = (bf16[192,256]{1,0:T(8,128)(2,1)S(1)}, bf16[192,256]{1,0:T(8,128)(2,1)}, u32[]{:S(2)}) copy-start(bf16[192,256]{1,0:T(8,128)(2,1)} %param.6) | copy-start | bytes 294916
  14.8 78.9 %copy-start.3 = (f32[1,512,256]{2,1,0:T(8,128)S(1)}, f32[1,512,256]{2,1,0:T(8,128)}, u32[]{:S(2)}) copy-start(f32[1,512,256]{2,1,0:T(8,128)} %param.8) | copy-start | bytes 1572868
  95.3 2.5 %copy-start.5 = (s32[64]{0:T(128)S(1)}, s32[64]{0:T(128)}, u32[]{:S(2)}) copy-start(s32[64]{0:T(128)} %param.9) | copy-start | bytes 772
  126.1 5.6 %copy-start.1 = (f32[8,64,4,64]{1,3,2,0:T(8,128)S(1)}, f32[8,64,4,64]{1,3,2,0:T(8,128)}, u32[]{:S(2)}) copy-start(f32[8,64,4,64]{1,3,2,0:T(8,128)} %fusion.51) | copy-start | bytes 1572868
Sparse Core Ops, SparseCore 0:
  10.2 31.8 all-gather.1
  44.4 49.3 reduce-scatter.1
where the time goes:
time: 147 us
  waiting for transfers between devices  75.3 us (51%)
  matrix products  24.2 us (16%)
  local copies, waits for them, and re-layouts  16 us (11%)
  between operations  14.2 us (10%)
  blocking collectives  10.9 us (7%)
  other arithmetic  6.36 us (4%)
    reduce_scatter x1, waiting for transfers between devices, on_device(): lax.psum_scatter(lax.dot_general(tokens, cotangent, (((0,), (0,)), ((), (...  48.1 us
    all_gather x1, waiting for transfers between devices, on_device(): lax.all_gather(weight_half, 'fsdp', axis=0, tiled=True)  27.2 us
    all_gather x1, blocking collectives, on_device(): gathered = lax.all_gather(flat_sent, 'rep', axis=0, tiled=True)  10.9 us
    unnamed x16, local copies, waits for them, and re-layouts  8.64 us
    dot_general x2, matrix products, on_device(): jnp.einsum('kn,akbl,lm->anbm', table, summed_full, table, precision=lax.P...  5.46 us
    dot_general x2, matrix products, on_device(): jnp.einsum('kn,akbl,lm->anbm', table, sent, table, precision=lax.Precisio...  4.42 us
    dot_general x1, matrix products, on_device(): lax.dot_general(tokens, cotangent, (((0,), (0,)), ((), ())), preferred_el...  3.61 us
    dot_general x1, matrix products, on_device(): lax.dot_general(cotangent, lax.all_gather(weight_half, 'fsdp', axis=0, ti...  3.58 us
  transfers between devices with their start and end apart: 2, of which 2 were waited for; matrix products, arithmetic and copies ran while one was open for 6% of the time, Pallas kernels for 0%

commit v1 on v0

v1 whole, which is shorter than its diff:
```python
import functools
import math

import jax
import jax.numpy as jnp
import numpy as np
from jax import lax
from jax.experimental import pallas as pl
from jax.experimental.pallas import tpu as pltpu
from jax.sharding import PartitionSpec as P


BLOCK = 64
SEL = 16
CORES = 2
LINE = 4

MOMENTUM_DECAY = 0.9
LEARN_RATE = 0.05
HIGHEST = lax.Precision.HIGHEST
BF16, F32 = jnp.bfloat16, jnp.float32


SMEM = pl.BlockSpec(memory_space=pltpu.SMEM)


def vmem(count):
    return [pl.BlockSpec(memory_space=pltpu.VMEM)] * count


def dct_rows(width):
    index = np.arange(BLOCK, dtype=np.float64)
    table = np.cos(math.pi * (2.0 * index[None, :] + 1.0) * index[:, None] / (2.0 * BLOCK))
    table *= math.sqrt(2.0 / BLOCK)
    table[0] *= math.sqrt(0.5)
    return np.tile(table, (1, width // BLOCK)).astype(np.float32)


def call(kernel, outs, in_specs, flops, nbytes, scratch=()):
    run = pl.pallas_call(
        kernel,
        out_shape=outs,
        in_specs=in_specs,
        out_specs=vmem(len(outs)),
        scratch_shapes=scratch,
        cost_estimate=pl.CostEstimate(flops=flops, bytes_accessed=nbytes, transcendentals=0),
        compiler_params=pltpu.CompilerParams(vmem_limit_bytes=32 << 20),
    )
    return run


def dot(a, b, dims, precision=None):
    return lax.dot_general(
        a, b, (dims, ((), ())), precision=precision, preferred_element_type=F32
    )


def position():
    member = lax.axis_index("fsdp")
    return lax.axis_index("rep"), member // CORES, lax.rem(member, CORES)


def wide(ref):
    return ref[...].astype(F32)


def start_kernel(order, rows, weight, cot, half, share, basis, coded_cot, table):
    for s in range(BLOCK):
        table[pl.ds(s, 1), :] = rows[pl.ds(order[s], 1), :]
    features = basis.shape[1]
    blocks = features // BLOCK
    rest = BLOCK - SEL
    for b in range(blocks):
        inside = lax.broadcasted_iota(jnp.int32, (BLOCK, features), 1) // BLOCK == b
        block = jnp.where(inside, table[...], 0.0)
        basis[pl.ds(b * SEL, SEL), :] = block[:SEL]
        basis[pl.ds(blocks * SEL + b * rest, rest), :] = block[SEL:]
    half[...] = weight[...].astype(BF16)
    part = share.shape[0]
    begin = pl.multiple_of(lax.axis_index("rep") * part, part)
    share[...] = weight[pl.ds(begin, part), :].astype(BF16)
    coded_cot[...] = dot(basis[...], wide(cot), ((1,), (1,)), HIGHEST).astype(BF16)


def partial_kernel(mine, theirs, own_tok, their_tok, *outs):
    codes, (turn, near, keep, own_code, own_rest) = outs[:-5], outs[-5:]
    _, chip, core = position()
    sent, columns = own_code.shape

    def total(mask):
        dest = chip ^ mask
        at = pl.ds(pl.multiple_of((CORES * dest + core) * columns, columns), columns)
        value = dot(mine[...], own_tok[:, at], ((1,), (0,)))
        return value + dot(theirs[...], their_tok[:, at], ((1,), (0,)))

    for mask, out in ((2, turn), (1, near), (3, keep)):
        value = total(mask)
        codes[mask - 1][...] = value[:sent].astype(BF16)
        out[...] = value[sent:].astype(out.dtype)
    value = total(0)
    own_code[...] = value[:sent]
    own_rest[...] = value[sent:]


def middle():
    _, chip, _ = position()
    return jnp.logical_and(chip > 0, chip < LINE - 1)


def old_kernel(basis, momentum, kept, coded):
    sent = basis[: coded.shape[0], :]
    old = MOMENTUM_DECAY * momentum[0]
    code = dot(sent, old, ((1,), (1,)), HIGHEST)
    coded[...] = code
    kept[...] = old - dot(code, sent, ((0,), (0,)), HIGHEST)


def join_kernel(*refs):
    part = refs[0].shape[0]
    for k, ref in enumerate(refs[:-1]):
        refs[-1][pl.ds(k * part, part), :] = ref[...]


def relay_kernel(keep, turned, out):
    passed = jnp.where(middle(), wide(turned), 0.0)
    out[...] = (keep[...] + passed).astype(out.dtype)


def code_kernel(scale, coded, own, *refs):
    total = own[...]
    for part in refs[:-1]:
        total += wide(part)
    refs[-1][...] = (coded[...] + scale * total).astype(BF16)


def moment_kernel(scale, basis, kept, own, near, turned, late, out):
    total = own[...] + wide(near) + wide(late)
    total += jnp.where(middle(), 0.0, wide(turned))
    rest = basis[basis.shape[0] - own.shape[0] :, :]
    grad = dot(total.astype(BF16), rest.astype(BF16), ((0,), (0,)))
    out[0] = kept[...] + scale * grad


def update_kernel(replicas, basis, weight, *refs):
    parts, (update, new_weight) = refs[:-2], refs[-2:]
    total = wide(parts[0])
    for part in parts[1:]:
        total += wide(part)
    sent = basis[: total.shape[0], :]
    value = dot(total, sent, ((0,), (0,)), HIGHEST) * (1.0 / replicas)
    update[...] = value
    new_weight[...] = weight[...] - LEARN_RATE * value


def input_kernel(chips, cot, *refs):
    pieces, out = refs[:-1], refs[-1]
    rep, chip, core = position()
    per_core = len(pieces) // CORES
    rows = pieces[0].shape[0]
    part = rows // (per_core - 1)
    for side in range(CORES):
        whose = lax.rem(core + side, CORES)
        own, parts = pieces[side * per_core], pieces[side * per_core + 1 : (side + 1) * per_core]
        begin = pl.multiple_of((CORES * chip + whose) * rows, rows)
        out[:, pl.ds(begin, rows)] = dot(cot[...], own[...], ((1,), (1,))).astype(out.dtype)
        for e, piece in enumerate(parts):
            value = dot(cot[...], piece[...], ((1,), (1,))).astype(out.dtype)
            for d in range(1, chips):
                begin = (CORES * (chip ^ d) + whose) * rows + (rep ^ e) * part
                at = pl.ds(pl.multiple_of(begin, part), part)
                out[:, at] = value[:, (d - 1) * part : d * part]


def tuned(tokens, cotangent, weight, momentum, column_order):
    members, replicas = lax.axis_size("fsdp"), lax.axis_size("rep")
    chips = members // CORES
    count, width = tokens.shape
    rows, features = weight.shape
    sent = features // BLOCK * SEL
    part = rows // replicas
    masks = range(1, chips)
    shape = jax.ShapeDtypeStruct

    def permute(x, axis, target):
        pairs = [(i, target(i)) for i in range(lax.axis_size(axis))]
        return lax.ppermute(x, axis, pairs)

    def swap(x):
        return permute(x, "fsdp", lambda i: i ^ 1)

    def chip_hop(x, target):
        return permute(x, "fsdp", lambda i: CORES * target(i // CORES) + i % CORES)

    def over_chips(x, mask):
        return chip_hop(x, lambda z: z ^ mask)

    def over_rep(x):
        return [permute(x, "rep", lambda i, e=e: i ^ e) for e in range(1, replicas)]

    their_tokens = swap(tokens)
    half, share, basis, mine = call(
        start_kernel,
        (
            shape((rows, features), BF16),
            shape((part, features), BF16),
            shape((features, features), F32),
            shape((features, count), BF16),
        ),
        [SMEM] + [pl.BlockSpec()] * 3,
        12 * features * features * count,
        32 * count * width,
        [pltpu.VMEM((BLOCK, features), F32)],
    )(column_order, dct_rows(features), weight, cotangent)
    theirs = swap(mine)
    shares = [over_chips(share, d) for d in masks]

    code, rest = shape((sent, rows), BF16), shape((features - sent, rows), BF16)
    *codes, turn, near, keep, own_code, own_rest = call(
        partial_kernel,
        (code,) * len(masks) + (rest, rest, shape(rest.shape, F32), shape(code.shape, F32), shape(rest.shape, F32)),
        vmem(4),
        2 * CORES * count * rows * chips * features,
        CORES * count * rows * chips * 2,
    )(mine, theirs, tokens, their_tokens)

    way = (1, 3, 0, 2)
    turned = chip_hop(turn, lambda z: way[z])
    codes = [over_chips(x, d) for d, x in zip(masks, codes)]
    near = over_chips(near, 1)
    (late,) = call(relay_kernel, (rest,), vmem(2), 0, rest.size * 8)(keep, turned)
    late = over_chips(late, LINE - 1)

    kept, coded = call(
        old_kernel,
        (shape((rows, features), F32), shape((sent, rows), F32)),
        vmem(2),
        24 * rows * features * sent,
        rows * features * 8,
    )(basis, momentum)
    scale = float(count * members) ** (-0.5)
    (packed,) = call(
        functools.partial(code_kernel, scale), (code,), vmem(2 + len(codes)), 0, sent * rows * 18
    )(coded, own_code, *codes)
    update, new_weight = call(
        functools.partial(update_kernel, replicas),
        (shape(weight.shape, F32),) * 2,
        vmem(2 + replicas),
        12 * rows * features * sent,
        rows * features * 12,
    )(basis, weight, packed, *over_rep(packed))
    (new_momentum,) = call(
        functools.partial(moment_kernel, scale),
        (shape(momentum.shape, F32),),
        vmem(6),
        2 * rows * features * features,
        rows * features * 16,
    )(basis, kept, own_rest, near, turned, late)

    (joined,) = call(
        join_kernel,
        (shape((part * len(shares), features), BF16),),
        vmem(len(shares)),
        0,
        part * len(shares) * features * 4,
    )(*shares)
    pieces = [half, joined] + over_rep(joined)
    pieces += [swap(x) for x in pieces]
    (input_grad,) = call(
        functools.partial(input_kernel, chips),
        (shape((count, width), BF16),),
        vmem(1 + len(pieces)),
        2 * count * width * features,
        2 * (count + features) * width,
    )(cotangent, *pieces)
    return input_grad, new_momentum, update, new_weight


def general(tokens, cotangent, weight, momentum, column_order):
    members, replicas = lax.axis_size("fsdp"), lax.axis_size("rep")
    features = weight.shape[1]
    whole = lax.all_gather(weight.astype(BF16), "fsdp", axis=0, tiled=True)
    input_grad = dot(cotangent, whole, ((1,), (1,))).astype(BF16)
    grad = lax.psum_scatter(
        dot(tokens, cotangent, ((0,), (0,))), "fsdp", scatter_dimension=0, tiled=True
    )
    moment = MOMENTUM_DECAY * momentum[0] + grad * float(tokens.shape[0] * members) ** (-0.5)
    lane_block = jnp.arange(features) // BLOCK
    chosen = jnp.asarray(dct_rows(features))[column_order[:SEL]]
    basis = jnp.concatenate(
        [jnp.where(lane_block == b, chosen, 0.0) for b in range(features // BLOCK)]
    )
    coded = dot(moment, basis, ((1,), (1,)), HIGHEST)
    new_momentum = (moment - dot(coded, basis, ((1,), (0,)), HIGHEST))[None]
    summed = jnp.sum(lax.all_gather(coded, "rep", axis=0), axis=0)
    update = dot(summed, basis, ((1,), (0,)), HIGHEST) / replicas
    return input_grad, new_momentum, update, weight - LEARN_RATE * update


def solution(mesh):
    in_specs = (
        P(("rep", "fsdp"), None),
        P(("rep", "fsdp"), None),
        P("fsdp", None),
        P("rep", "fsdp", None),
        P(),
    )
    out_specs = (P(("rep", "fsdp"), None), P("rep", "fsdp", None), P("fsdp", None), P("fsdp", None))
    members, replicas = mesh.shape["fsdp"], mesh.shape["rep"]
    line = members == LINE * CORES and replicas == LINE

    def on_device(*args):
        if not line:
            return general(*args)
        return tuned(*args)

    return jax.shard_map(
        on_device, mesh=mesh, in_specs=in_specs, out_specs=out_specs, check_vma=False
    )
```

time: 147 us -> 55.6 us (0.38)
  waiting for transfers between devices: 75.3 us -> 17.9 us
  matrix products: 24.2 us -> 0 us
  starting transfers between devices: 0.08 us -> 24 us
  between operations: 14.2 us -> 0.73 us
  local copies, waits for them, and re-layouts: 16 us -> 4.85 us
  blocking collectives: 10.9 us -> 0 us
  Pallas kernels: 0 us -> 7.85 us
  other arithmetic: 6.36 us -> 0 us
    reduce_scatter x1 -> x0, waiting for transfers between devices: 48.1 us -> none  [on_device(): lax.psum_scatter(lax.dot_general(tokens, cotangent, (((0,), (0,)), ((), (...]
    all_gather x1 -> x0, waiting for transfers between devices: 27.2 us -> none  [on_device(): lax.all_gather(weight_half, 'fsdp', axis=0, tiled=True)]
    dot_general x11 -> x0, matrix products: 24.2 us -> none  [the longest x2 5.46 us: on_device(): jnp.einsum('kn,akbl,lm->anbm', table, summed_full, table, precision=lax.P...]
    ppermute x0 -> x22, starting transfers between devices: none -> 24 us  [permute(): return lax.ppermute(x, axis, pairs)]
    ppermute x0 -> x22, waiting for transfers between devices: none -> 17.9 us  [permute(): return lax.ppermute(x, axis, pairs)]
    all_gather x1 -> x0, blocking collectives: 10.9 us -> none  [on_device(): gathered = lax.all_gather(flat_sent, 'rep', axis=0, tiled=True)]
    pallas_call x0 -> x9, Pallas kernels: none -> 7.85 us  [the longest x1 2.09 us: tuned(): call(functools.partial(input_kernel, chips), (shape((count, width), BF16)...]
    unnamed x16, local copies, waits for them, and re-layouts: 8.64 us -> 4.85 us
  transfers between devices with their start and end apart: 2 -> 22, of which waited for: 2 -> 9; matrix products, arithmetic and copies ran while one was open for 6% -> 0% of each run, Pallas kernels for 0% -> 12%
where the time goes in v1:
time: 55.6 us; the launch traced here: 55.3 us
  starting transfers between devices  24 us (43%)
  waiting for transfers between devices  17.9 us (32%)
  Pallas kernels  7.85 us (14%)
  local copies, waits for them, and re-layouts  4.85 us (9%)
  between operations  0.73 us (1%)
    ppermute x22, starting transfers between devices, permute(): return lax.ppermute(x, axis, pairs)  24 us
    ppermute x22, waiting for transfers between devices, permute(): return lax.ppermute(x, axis, pairs)  17.9 us
    unnamed x16, local copies, waits for them, and re-layouts  4.85 us
    pallas_call x1, Pallas kernels, tuned(): call(functools.partial(input_kernel, chips), (shape((count, width), BF16)...  2.09 us
    pallas_call x1, Pallas kernels, tuned(): call(functools.partial(update_kernel, replicas), (shape(weight.shape, F32...  1.6 us
    pallas_call x1, Pallas kernels, tuned(): call(old_kernel, (shape((rows, features), F32), shape((sent, rows), F32))...  1.23 us
  transfers between devices with their start and end apart: 22, of which 9 were waited for; matrix products, arithmetic and copies ran while one was open for 0% of the time, Pallas kernels for 12%

profile of v1, /device:TPU:0, one launch (start us, length us, event | category | flops | bytes accessed | tf_op | source)
XLA Modules:
  0.0 55.3 jit_solution(14744565096944442)
XLA Ops:
  0.6 0.6 %collective-permute-start.12 = (bf16[192,4096]{1,0:T(8,128)(2,1)}, bf16[192,4096]{1,0:T(8,128)(2,1)S(1)}, u32[]{:S(2)}, u32[]{:S(2)}) collective-permute-start(bf16[192,4096]{1,0:T(8,128)(2,1)} %own_tok.1), channel_id=1, source_target_pairs={{0,1},{1,0},{2,3},{3,2},{4,5},{5,4},{6,7},{7,6},{8,9},{9,8},{10,11... | collective-permute-start | bytes 4718600 | tf_op jit(solution)/shard_map/ppermute | solution.py:186
  1.2 1.0 %copy-done = f32[512,256]{1,0:T(8,128)S(1)} copy-done((f32[512,256]{1,0:T(8,128)S(1)}, f32[512,256]{1,0:T(8,128)}, u32[]{:S(2)}) %copy-start) | copy-done | bytes 524312
  2.2 0.9 %copy-done.4 = bf16[192,256]{1,0:T(8,128)(2,1)S(1)} copy-done((bf16[192,256]{1,0:T(8,128)(2,1)S(1)}, bf16[192,256]{1,0:T(8,128)(2,1)}, u32[]{:S(2)}) %copy-start.4) | copy-done | bytes 98328
  3.1 0.8 %copy-done.6 = f32[64,256]{1,0:T(8,128)S(1)} copy-done((f32[64,256]{1,0:T(8,128)S(1)}, f32[64,256]{1,0:T(8,128)}, u32[]{:S(2)}) %copy-start.6) | copy-done | bytes 65560
  4.0 0.7 %copy-done.7 = s32[64]{0:T(128)S(1)} copy-done((s32[64]{0:T(128)S(1)}, s32[64]{0:T(128)}, u32[]{:S(2)}) %copy-start.7) | copy-done | bytes 280
  4.6 1.0 %shard_map.93 = (bf16[512,256]{1,0:T(8,128)(2,1)S(1)}, bf16[128,256]{1,0:T(8,128)(2,1)S(1)}, f32[256,256]{1,0:T(8,128)S(1)}, bf16[256,192]{1,0:T(8,128)(2,1)S(1)}) custom-call(s32[64]{0:T(128)S(1)} %copy-done.7, f32[64,256]{1,0:T(8,128)S(1)} %copy-done.6, f32[512,256]{1,0:T(8,128)S(1)} %copy-done, bf16[192,256]{1,0:T(8,128)(2,1)S(1)} %copy-done.4), custom_call_target="tpu_custom_call" | custom-call | flops 150994944 | bytes 25165824 | tf_op jit(solution)/shard_map/pallas_call | solution.py:201
  5.6 2.6 %collective-permute-start = (bf16[128,256]{1,0:T(8,128)(2,1)S(1)}, bf16[128,256]{1,0:T(8,128)(2,1)S(1)}, u32[]{:S(2)}, u32[]{:S(2)}) collective-permute-start(bf16[128,256]{1,0:T(8,128)(2,1)S(1)} %get-tuple-element.21), channel_id=1, source_target_pairs={{0,2},{1,3},{2,0},{3,1},{4,6},{5,7},{6,4},{7,5},{8,10},{9,11},{10,... | collective-permute-start | bytes 196616 | tf_op jit(solution)/shard_map/ppermute | solution.py:186
  8.3 2.6 %collective-permute-start.1 = (bf16[128,256]{1,0:T(8,128)(2,1)S(1)}, bf16[128,256]{1,0:T(8,128)(2,1)S(1)}, u32[]{:S(2)}, u32[]{:S(2)}) collective-permute-start(bf16[128,256]{1,0:T(8,128)(2,1)S(1)} %get-tuple-element.21), channel_id=1, source_target_pairs={{0,4},{1,5},{2,6},{3,7},{4,0},{5,1},{6,2},{7,3},{8,12},{9,13},{10,... | collective-permute-start | bytes 196616 | tf_op jit(solution)/shard_map/ppermute | solution.py:186
  10.9 0.2 collective-permute-done.refs_0_
  11.0 4.3 %collective-permute-done.1.refs_1_ = bf16[128,256]{1,0:T(8,128)(2,1)S(1)} collective-permute-done((bf16[128,256]{1,0:T(8,128)(2,1)S(1)}, bf16[128,256]{1,0:T(8,128)(2,1)S(1)}, u32[]{:S(2)}, u32[]{:S(2)}) %collective-permute-start.1) | collective-permute-done | bytes 65568 | tf_op jit(solution)/shard_map/ppermute | solution.py:186
  15.3 1.6 %collective-permute-done.2.refs_2_ = bf16[128,256]{1,0:T(8,128)(2,1)S(1)} collective-permute-done((bf16[128,256]{1,0:T(8,128)(2,1)S(1)}, bf16[128,256]{1,0:T(8,128)(2,1)S(1)}, u32[]{:S(2)}, u32[]{:S(2)}) %collective-permute-start.2) | collective-permute-done | bytes 65568 | tf_op jit(solution)/shard_map/ppermute | solution.py:186
  17.0 2.5 %collective-permute-start.5 = (bf16[384,256]{1,0:T(8,128)(2,1)S(1)}, bf16[384,256]{1,0:T(8,128)(2,1)S(1)}, u32[]{:S(2)}, u32[]{:S(2)}) collective-permute-start(bf16[384,256]{1,0:T(8,128)(2,1)S(1)} %shard_map.94.refs_1_), channel_id=1, source_target_pairs={{0,24},{8,16},{16,8},{24,0},{1,25},{9,17},{17,9},{25,1},{2,26},{10... | collective-permute-start | bytes 589832 | tf_op jit(solution)/shard_map/ppermute | solution.py:186
  19.5 0.0 collective-permute-start.11
  19.5 0.5 collective-permute-start.6
  20.0 0.5 collective-permute-start.3
  20.5 0.3 collective-permute-done.11.theirs
  20.8 0.5 collective-permute-start.4
  21.3 0.0 collective-permute-done.12.their_tok
  21.3 0.0 collective-permute-start.7
  21.3 1.4 %copy-done.2 = bf16[192,4096]{1,0:T(8,128)(2,1)S(1)} copy-done((bf16[192,4096]{1,0:T(8,128)(2,1)S(1)}, bf16[192,4096]{1,0:T(8,128)(2,1)}, u32[]{:S(2)}) %copy-start.2) | copy-done | bytes 1572888
  22.7 0.7 %shard_map.97 = (bf16[64,512]{1,0:T(8,128)(2,1)S(1)}, bf16[64,512]{1,0:T(8,128)(2,1)S(1)}, bf16[64,512]{1,0:T(8,128)(2,1)S(1)}, bf16[192,512]{1,0:T(8,128)(2,1)S...) custom-call(bf16[256,192]{1,0:T(8,128)(2,1)S(1)} %get-tuple-element., ...), custom_call_target="tpu_custom_call" | custom-call | flops 402653184 | bytes 1572864 | tf_op jit(solution)/shard_map/pallas_call | solution.py:218
  23.4 0.0 copy-start.5
  23.5 1.3 %collective-permute-done.5.refs_4_ = bf16[384,256]{1,0:T(8,128)(2,1)S(1)} collective-permute-done((bf16[384,256]{1,0:T(8,128)(2,1)S(1)}, bf16[384,256]{1,0:T(8,128)(2,1)S(1)}, u32[]{:S(2)}, u32[]{:S(2)}) %collective-permute-start.5) | collective-permute-done | bytes 196640 | tf_op jit(solution)/shard_map/ppermute | solution.py:186
  24.7 2.3 %collective-permute-start.14 = (bf16[192,512]{1,0:T(8,128)(2,1)S(1)}, bf16[192,512]{1,0:T(8,128)(2,1)S(1)}, u32[]{:S(2)}, u32[]{:S(2)}) collective-permute-start(bf16[192,512]{1,0:T(8,128)(2,1)S(1)} %get-tuple-element.27), channel_id=1, source_target_pairs={{0,2},{1,3},{2,6},{3,7},{4,0},{5,1},{6,4},{7,5},{8,10},{9,11},{10,... | collective-permute-start | bytes 589832 | tf_op jit(solution)/shard_map/ppermute | solution.py:186
  27.0 0.9 %collective-permute-done.3.refs_2_ = bf16[384,256]{1,0:T(8,128)(2,1)S(1)} collective-permute-done((bf16[384,256]{1,0:T(8,128)(2,1)S(1)}, bf16[384,256]{1,0:T(8,128)(2,1)S(1)}, u32[]{:S(2)}, u32[]{:S(2)}) %collective-permute-start.3) | collective-permute-done | bytes 196640 | tf_op jit(solution)/shard_map/ppermute | solution.py:186
  27.9 2.1 %collective-permute-start.16 = (bf16[64,512]{1,0:T(8,128)(2,1)S(1)}, bf16[64,512]{1,0:T(8,128)(2,1)S(1)}, u32[]{:S(2)}, u32[]{:S(2)}) collective-permute-start(bf16[64,512]{1,0:T(8,128)(2,1)S(1)} %get-tuple-element.31), channel_id=1, source_target_pairs={{0,2},{1,3},{2,0},{3,1},{4,6},{5,7},{6,4},{7,5},{8,10},{9,11},{10,... | collective-permute-start | bytes 196616 | tf_op jit(solution)/shard_map/ppermute | solution.py:186
  30.0 0.0 collective-permute-done.4.refs_3_
  30.0 0.5 collective-permute-start.8
  30.5 0.0 collective-permute-done.6.refs_5_
  30.5 0.1 collective-permute-start.9
  30.5 2.6 %collective-permute-done.16.refs_0_ = bf16[64,512]{1,0:T(8,128)(2,1)S(1)} collective-permute-done((bf16[64,512]{1,0:T(8,128)(2,1)S(1)}, bf16[64,512]{1,0:T(8,128)(2,1)S(1)}, u32[]{:S(2)}, u32[]{:S(2)}) %collective-permute-start.16) | collective-permute-done | bytes 65568 | tf_op jit(solution)/shard_map/ppermute | solution.py:186
  33.1 1.4 %collective-permute-start.17 = (bf16[64,512]{1,0:T(8,128)(2,1)S(1)}, bf16[64,512]{1,0:T(8,128)(2,1)S(1)}, u32[]{:S(2)}, u32[]{:S(2)}) collective-permute-start(bf16[64,512]{1,0:T(8,128)(2,1)S(1)} %get-tuple-element.32), channel_id=1, source_target_pairs={{0,4},{1,5},{2,6},{3,7},{4,0},{5,1},{6,2},{7,3},{8,12},{9,13},{10,... | collective-permute-start | bytes 196616 | tf_op jit(solution)/shard_map/ppermute | solution.py:186
  34.6 0.0 collective-permute-done.14.turned
  34.6 2.0 %collective-permute-start.18 = (bf16[64,512]{1,0:T(8,128)(2,1)S(1)}, bf16[64,512]{1,0:T(8,128)(2,1)S(1)}, u32[]{:S(2)}, u32[]{:S(2)}) collective-permute-start(bf16[64,512]{1,0:T(8,128)(2,1)S(1)} %get-tuple-element.33), channel_id=1, source_target_pairs={{0,6},{1,7},{2,4},{3,5},{4,2},{5,3},{6,0},{7,1},{8,14},{9,15},{10,... | collective-permute-start | bytes 196616 | tf_op jit(solution)/shard_map/ppermute | solution.py:186
  36.6 0.1 shard_map.98
  36.6 4.5 %collective-permute-done.17.refs_1_ = bf16[64,512]{1,0:T(8,128)(2,1)S(1)} collective-permute-done((bf16[64,512]{1,0:T(8,128)(2,1)S(1)}, bf16[64,512]{1,0:T(8,128)(2,1)S(1)}, u32[]{:S(2)}, u32[]{:S(2)}) %collective-permute-start.17) | collective-permute-done | bytes 65568 | tf_op jit(solution)/shard_map/ppermute | solution.py:186
  41.1 2.2 %collective-permute-start.15 = (bf16[192,512]{1,0:T(8,128)(2,1)S(1)}, bf16[192,512]{1,0:T(8,128)(2,1)S(1)}, u32[]{:S(2)}, u32[]{:S(2)}) collective-permute-start(bf16[192,512]{1,0:T(8,128)(2,1)S(1)} %shard_map.98), channel_id=1, source_target_pairs={{0,6},{1,7},{2,4},{3,5},{4,2},{5,3},{6,0},{7,1},{8,14},{9,15},{10,... | collective-permute-start | bytes 589832 | tf_op jit(solution)/shard_map/ppermute | solution.py:186
  43.3 1.2 %shard_map.96 = (f32[512,256]{1,0:T(8,128)S(1)}, f32[64,512]{1,0:T(8,128)S(1)}) custom-call(f32[256,256]{1,0:T(8,128)S(1)} %get-tuple-element.22.basis, f32[1,512,256]{2,1,0:T(8,128)S(1)} %copy-done.3), custom_call_target="tpu_custom_call" | custom-call | flops 201326592 | bytes 1048576 | tf_op jit(solution)/shard_map/pallas_call | solution.py:233
  44.6 0.0 copy-start.1
  44.6 0.0 collective-permute-done.10.refs_9_
  44.6 1.0 %collective-permute-start.19 = (bf16[64,512]{1,0:T(8,128)(2,1)S(1)}, bf16[64,512]{1,0:T(8,128)(2,1)S(1)}, u32[]{:S(2)}, u32[]{:S(2)}) collective-permute-start(bf16[64,512]{1,0:T(8,128)(2,1)S(1)} %shard_map.100.refs_0_), channel_id=1, source_target_pairs={{0,8},{8,0},{16,24},{24,16},{1,9},{9,1},{17,25},{25,17},{2,10},{10... | collective-permute-start | bytes 196616 | tf_op jit(solution)/shard_map/ppermute | solution.py:186
  45.6 0.0 collective-permute-done.8.refs_7_
  45.6 1.8 %collective-permute-start.20 = (bf16[64,512]{1,0:T(8,128)(2,1)S(1)}, bf16[64,512]{1,0:T(8,128)(2,1)S(1)}, u32[]{:S(2)}, u32[]{:S(2)}) collective-permute-start(bf16[64,512]{1,0:T(8,128)(2,1)S(1)} %shard_map.100.refs_0_), channel_id=1, source_target_pairs={{0,16},{8,24},{16,0},{24,8},{1,17},{9,25},{17,1},{25,9},{2,18},{10... | collective-permute-start | bytes 196616 | tf_op jit(solution)/shard_map/ppermute | solution.py:186
  47.4 0.8 %collective-permute-start.21 = (bf16[64,512]{1,0:T(8,128)(2,1)S(1)}, bf16[64,512]{1,0:T(8,128)(2,1)S(1)}, u32[]{:S(2)}, u32[]{:S(2)}) collective-permute-start(bf16[64,512]{1,0:T(8,128)(2,1)S(1)} %shard_map.100.refs_0_), channel_id=1, source_target_pairs={{0,24},{8,16},{16,8},{24,0},{1,25},{9,17},{17,9},{25,1},{2,26},{10... | collective-permute-start | bytes 196616 | tf_op jit(solution)/shard_map/ppermute | solution.py:186
  48.2 2.1 %shard_map.95 = bf16[192,4096]{1,0:T(8,128)(2,1)} custom-call(bf16[192,256]{1,0:T(8,128)(2,1)S(1)} %copy-done.5, bf16[512,256]{1,0:T(8,128)(2,1)S(1)} %get-tuple-element.20.refs_0_, bf16[384,256]{1,0:T(8,128)(2,1)S(1)} %shard_map.94.refs_1_, bf16[384,256]{1,0:T(8,128)(2,1)S(1)} %collective-permute-done.3.refs_2_, ...), custom_call_target="tpu_custom_call" | custom-call | flops 402653184 | bytes 3670016 | tf_op jit(solution)/shard_map/pallas_call | solution.py:268
  50.3 2.3 %collective-permute-done.21.refs_3_ = bf16[64,512]{1,0:T(8,128)(2,1)S(1)} collective-permute-done((bf16[64,512]{1,0:T(8,128)(2,1)S(1)}, bf16[64,512]{1,0:T(8,128)(2,1)S(1)}, u32[]{:S(2)}, u32[]{:S(2)}) %collective-permute-start.21) | collective-permute-done | bytes 65568 | tf_op jit(solution)/shard_map/ppermute | solution.py:186
  52.6 1.6 %shard_map.101 = (f32[512,256]{1,0:T(8,128)}, f32[512,256]{1,0:T(8,128)}) custom-call(f32[256,256]{1,0:T(8,128)S(1)} %get-tuple-element.22.basis, f32[512,256]{1,0:T(8,128)S(1)} %copy-done.1, bf16[64,512]{1,0:T(8,128)(2,1)S(1)} %shard_map.100.refs_0_, bf16[64,512]{1,0:T(8,128)(2,1)S(1)} %collective-permute-done.19.refs_1_, ...), custom_call_target="tpu_custom_call" | custom-call | flops 100663296 | bytes 1572864 | tf_op jit(solution)/shard_map/pallas_call | solution.py:244
  54.2 1.1 %shard_map.99 = f32[1,512,256]{2,1,0:T(8,128)} custom-call(f32[256,256]{1,0:T(8,128)S(1)} %get-tuple-element.22.basis, f32[512,256]{1,0:T(8,128)S(1)} %get-tuple-element.23.kept, f32[192,512]{1,0:T(8,128)S(1)} %get-tuple-element.25.own, bf16[192,512]{1,0:T(8,128)(2,1)S(1)} %collective-permute-done.13.near, ...), custom_call_target="tpu_custom_call" | custom-call | flops 67108864 | bytes 2097152 | tf_op jit(solution)/shard_map/pallas_call | solution.py:251
  (21 shorter events, 0.1 us)
Async XLA Ops:
  0.6 20.7 %collective-permute-start.12 = (bf16[192,4096]{1,0:T(8,128)(2,1)}, bf16[192,4096]{1,0:T(8,128)(2,1)S(1)}, u32[]{:S(2)}, u32[]{:S(2)}) collective-permute-start(bf16[192,4096]{1,0:T(8,128)(2,1)} %own_tok.1), channel_id=1, source_target_pairs={{0,1},{1,0},{2,3},{3,2},{4,5},{5,4},{6,7},{7,6},{8,9},{9,8},{10,11... | collective-permute-start | bytes 4718600 | tf_op jit(solution)/shard_map/ppermute | solution.py:186
  1.2 1.0 %copy-start = (f32[512,256]{1,0:T(8,128)S(1)}, f32[512,256]{1,0:T(8,128)}, u32[]{:S(2)}) copy-start(f32[512,256]{1,0:T(8,128)} %weight.3) | copy-start | bytes 1572868
  2.2 0.9 %copy-start.4 = (bf16[192,256]{1,0:T(8,128)(2,1)S(1)}, bf16[192,256]{1,0:T(8,128)(2,1)}, u32[]{:S(2)}) copy-start(bf16[192,256]{1,0:T(8,128)(2,1)} %cot.3) | copy-start | bytes 294916
  3.1 0.8 %copy-start.6 = (f32[64,256]{1,0:T(8,128)S(1)}, f32[64,256]{1,0:T(8,128)}, u32[]{:S(2)}) copy-start(f32[64,256]{1,0:T(8,128)} %constant.2.clone.rows) | copy-start | bytes 196612
  4.0 0.7 %copy-start.7 = (s32[64]{0:T(128)S(1)}, s32[64]{0:T(128)}, u32[]{:S(2)}) copy-start(s32[64]{0:T(128)} %order.1) | copy-start | bytes 772
  5.6 5.4 %collective-permute-start = (bf16[128,256]{1,0:T(8,128)(2,1)S(1)}, bf16[128,256]{1,0:T(8,128)(2,1)S(1)}, u32[]{:S(2)}, u32[]{:S(2)}) collective-permute-start(bf16[128,256]{1,0:T(8,128)(2,1)S(1)} %get-tuple-element.21), channel_id=1, source_target_pairs={{0,2},{1,3},{2,0},{3,1},{4,6},{5,7},{6,4},{7,5},{8,10},{9,11},{10,... | collective-permute-start | bytes 196616 | tf_op jit(solution)/shard_map/ppermute | solution.py:186
  8.3 7.0 %collective-permute-start.1 = (bf16[128,256]{1,0:T(8,128)(2,1)S(1)}, bf16[128,256]{1,0:T(8,128)(2,1)S(1)}, u32[]{:S(2)}, u32[]{:S(2)}) collective-permute-start(bf16[128,256]{1,0:T(8,128)(2,1)S(1)} %get-tuple-element.21), channel_id=1, source_target_pairs={{0,4},{1,5},{2,6},{3,7},{4,0},{5,1},{6,2},{7,3},{8,12},{9,13},{10,... | collective-permute-start | bytes 196616 | tf_op jit(solution)/shard_map/ppermute | solution.py:186
  10.9 6.1 %collective-permute-start.2 = (bf16[128,256]{1,0:T(8,128)(2,1)S(1)}, bf16[128,256]{1,0:T(8,128)(2,1)S(1)}, u32[]{:S(2)}, u32[]{:S(2)}) collective-permute-start(bf16[128,256]{1,0:T(8,128)(2,1)S(1)} %get-tuple-element.21), channel_id=1, source_target_pairs={{0,6},{1,7},{2,4},{3,5},{4,2},{5,3},{6,0},{7,1},{8,14},{9,15},{10,... | collective-permute-start | bytes 196616 | tf_op jit(solution)/shard_map/ppermute | solution.py:186
  17.0 7.8 %collective-permute-start.5 = (bf16[384,256]{1,0:T(8,128)(2,1)S(1)}, bf16[384,256]{1,0:T(8,128)(2,1)S(1)}, u32[]{:S(2)}, u32[]{:S(2)}) collective-permute-start(bf16[384,256]{1,0:T(8,128)(2,1)S(1)} %shard_map.94.refs_1_), channel_id=1, source_target_pairs={{0,24},{8,16},{16,8},{24,0},{1,25},{9,17},{17,9},{25,1},{2,26},{10... | collective-permute-start | bytes 589832 | tf_op jit(solution)/shard_map/ppermute | solution.py:186
  19.5 1.3 %collective-permute-start.11 = (bf16[256,192]{1,0:T(8,128)(2,1)S(1)}, bf16[256,192]{1,0:T(8,128)(2,1)S(1)}, u32[]{:S(2)}, u32[]{:S(2)}) collective-permute-start(bf16[256,192]{1,0:T(8,128)(2,1)S(1)} %get-tuple-element.24.mine), channel_id=1, source_target_pairs={{0,1},{1,0},{2,3},{3,2},{4,5},{5,4},{6,7},{7,6},{8,9},{9,8},{10,11... | collective-permute-start | bytes 294920 | tf_op jit(solution)/shard_map/ppermute | solution.py:186
  19.5 11.0 %collective-permute-start.6 = (bf16[512,256]{1,0:T(8,128)(2,1)S(1)}, bf16[512,256]{1,0:T(8,128)(2,1)S(1)}, u32[]{:S(2)}, u32[]{:S(2)}) collective-permute-start(bf16[512,256]{1,0:T(8,128)(2,1)S(1)} %get-tuple-element.20.refs_0_), channel_id=1, source_target_pairs={{0,1},{1,0},{2,3},{3,2},{4,5},{5,4},{6,7},{7,6},{8,9},{9,8},{10,11... | collective-permute-start | bytes 786440 | tf_op jit(solution)/shard_map/ppermute | solution.py:186
  20.0 7.9 %collective-permute-start.3 = (bf16[384,256]{1,0:T(8,128)(2,1)S(1)}, bf16[384,256]{1,0:T(8,128)(2,1)S(1)}, u32[]{:S(2)}, u32[]{:S(2)}) collective-permute-start(bf16[384,256]{1,0:T(8,128)(2,1)S(1)} %shard_map.94.refs_1_), channel_id=1, source_target_pairs={{0,8},{8,0},{16,24},{24,16},{1,9},{9,1},{17,25},{25,17},{2,10},{10... | collective-permute-start | bytes 589832 | tf_op jit(solution)/shard_map/ppermute | solution.py:186
  20.8 9.1 %collective-permute-start.4 = (bf16[384,256]{1,0:T(8,128)(2,1)S(1)}, bf16[384,256]{1,0:T(8,128)(2,1)S(1)}, u32[]{:S(2)}, u32[]{:S(2)}) collective-permute-start(bf16[384,256]{1,0:T(8,128)(2,1)S(1)} %shard_map.94.refs_1_), channel_id=1, source_target_pairs={{0,16},{8,24},{16,0},{24,8},{1,17},{9,25},{17,1},{25,9},{2,18},{10... | collective-permute-start | bytes 589832 | tf_op jit(solution)/shard_map/ppermute | solution.py:186
  21.3 8.6 %collective-permute-start.7 = (bf16[384,256]{1,0:T(8,128)(2,1)S(1)}, bf16[384,256]{1,0:T(8,128)(2,1)S(1)}, u32[]{:S(2)}, u32[]{:S(2)}) collective-permute-start(bf16[384,256]{1,0:T(8,128)(2,1)S(1)} %shard_map.94.refs_1_), channel_id=1, source_target_pairs={{0,1},{1,0},{2,3},{3,2},{4,5},{5,4},{6,7},{7,6},{8,9},{9,8},{10,11... | collective-permute-start | bytes 589832 | tf_op jit(solution)/shard_map/ppermute | solution.py:186
  21.3 1.4 %copy-start.2 = (bf16[192,4096]{1,0:T(8,128)(2,1)S(1)}, bf16[192,4096]{1,0:T(8,128)(2,1)}, u32[]{:S(2)}) copy-start(bf16[192,4096]{1,0:T(8,128)(2,1)} %own_tok.1) | copy-start | bytes 4718596
  22.7 20.6 %copy-start.3 = (f32[1,512,256]{2,1,0:T(8,128)S(1)}, f32[1,512,256]{2,1,0:T(8,128)}, u32[]{:S(2)}) copy-start(f32[1,512,256]{2,1,0:T(8,128)} %momentum.1) | copy-start | bytes 1572868
  23.4 24.8 %copy-start.5 = (bf16[192,256]{1,0:T(8,128)(2,1)S(1)}, bf16[192,256]{1,0:T(8,128)(2,1)}, u32[]{:S(2)}) copy-start(bf16[192,256]{1,0:T(8,128)(2,1)} %cot.3) | copy-start | bytes 294916
  24.7 9.9 %collective-permute-start.14 = (bf16[192,512]{1,0:T(8,128)(2,1)S(1)}, bf16[192,512]{1,0:T(8,128)(2,1)S(1)}, u32[]{:S(2)}, u32[]{:S(2)}) collective-permute-start(bf16[192,512]{1,0:T(8,128)(2,1)S(1)} %get-tuple-element.27), channel_id=1, source_target_pairs={{0,2},{1,3},{2,6},{3,7},{4,0},{5,1},{6,4},{7,5},{8,10},{9,11},{10,... | collective-permute-start | bytes 589832 | tf_op jit(solution)/shard_map/ppermute | solution.py:186
  27.9 5.3 %collective-permute-start.16 = (bf16[64,512]{1,0:T(8,128)(2,1)S(1)}, bf16[64,512]{1,0:T(8,128)(2,1)S(1)}, u32[]{:S(2)}, u32[]{:S(2)}) collective-permute-start(bf16[64,512]{1,0:T(8,128)(2,1)S(1)} %get-tuple-element.31), channel_id=1, source_target_pairs={{0,2},{1,3},{2,0},{3,1},{4,6},{5,7},{6,4},{7,5},{8,10},{9,11},{10,... | collective-permute-start | bytes 196616 | tf_op jit(solution)/shard_map/ppermute | solution.py:186
  30.0 14.7 %collective-permute-start.10 = (bf16[384,256]{1,0:T(8,128)(2,1)S(1)}, bf16[384,256]{1,0:T(8,128)(2,1)S(1)}, u32[]{:S(2)}, u32[]{:S(2)}) collective-permute-start(bf16[384,256]{1,0:T(8,128)(2,1)S(1)} %collective-permute-done.5.refs_4_), channel_id=1, source_target_pairs={{0,1},{1,0},{2,3},{3,2},{4,5},{5,4},{6,7},{7,6},{8,9},{9,8},{10,11... | collective-permute-start | bytes 589832 | tf_op jit(solution)/shard_map/ppermute | solution.py:186
  30.0 15.7 %collective-permute-start.8 = (bf16[384,256]{1,0:T(8,128)(2,1)S(1)}, bf16[384,256]{1,0:T(8,128)(2,1)S(1)}, u32[]{:S(2)}, u32[]{:S(2)}) collective-permute-start(bf16[384,256]{1,0:T(8,128)(2,1)S(1)} %collective-permute-done.3.refs_2_), channel_id=1, source_target_pairs={{0,1},{1,0},{2,3},{3,2},{4,5},{5,4},{6,7},{7,6},{8,9},{9,8},{10,11... | collective-permute-start | bytes 589832 | tf_op jit(solution)/shard_map/ppermute | solution.py:186
  30.5 16.9 %collective-permute-start.9 = (bf16[384,256]{1,0:T(8,128)(2,1)S(1)}, bf16[384,256]{1,0:T(8,128)(2,1)S(1)}, u32[]{:S(2)}, u32[]{:S(2)}) collective-permute-start(bf16[384,256]{1,0:T(8,128)(2,1)S(1)} %collective-permute-done.4.refs_3_), channel_id=1, source_target_pairs={{0,1},{1,0},{2,3},{3,2},{4,5},{5,4},{6,7},{7,6},{8,9},{9,8},{10,11... | collective-permute-start | bytes 589832 | tf_op jit(solution)/shard_map/ppermute | solution.py:186
  33.1 8.0 %collective-permute-start.17 = (bf16[64,512]{1,0:T(8,128)(2,1)S(1)}, bf16[64,512]{1,0:T(8,128)(2,1)S(1)}, u32[]{:S(2)}, u32[]{:S(2)}) collective-permute-start(bf16[64,512]{1,0:T(8,128)(2,1)S(1)} %get-tuple-element.32), channel_id=1, source_target_pairs={{0,4},{1,5},{2,6},{3,7},{4,0},{5,1},{6,2},{7,3},{8,12},{9,13},{10,... | collective-permute-start | bytes 196616 | tf_op jit(solution)/shard_map/ppermute | solution.py:186
  34.6 6.6 %collective-permute-start.18 = (bf16[64,512]{1,0:T(8,128)(2,1)S(1)}, bf16[64,512]{1,0:T(8,128)(2,1)S(1)}, u32[]{:S(2)}, u32[]{:S(2)}) collective-permute-start(bf16[64,512]{1,0:T(8,128)(2,1)S(1)} %get-tuple-element.33), channel_id=1, source_target_pairs={{0,6},{1,7},{2,4},{3,5},{4,2},{5,3},{6,0},{7,1},{8,14},{9,15},{10,... | collective-permute-start | bytes 196616 | tf_op jit(solution)/shard_map/ppermute | solution.py:186
  41.1 13.1 %collective-permute-start.13 = (bf16[192,512]{1,0:T(8,128)(2,1)S(1)}, bf16[192,512]{1,0:T(8,128)(2,1)S(1)}, u32[]{:S(2)}, u32[]{:S(2)}) collective-permute-start(bf16[192,512]{1,0:T(8,128)(2,1)S(1)} %get-tuple-element.26), channel_id=1, source_target_pairs={{0,2},{1,3},{2,0},{3,1},{4,6},{5,7},{6,4},{7,5},{8,10},{9,11},{10,... | collective-permute-start | bytes 589832 | tf_op jit(solution)/shard_map/ppermute | solution.py:186
  41.1 13.1 %collective-permute-start.15 = (bf16[192,512]{1,0:T(8,128)(2,1)S(1)}, bf16[192,512]{1,0:T(8,128)(2,1)S(1)}, u32[]{:S(2)}, u32[]{:S(2)}) collective-permute-start(bf16[192,512]{1,0:T(8,128)(2,1)S(1)} %shard_map.98), channel_id=1, source_target_pairs={{0,6},{1,7},{2,4},{3,5},{4,2},{5,3},{6,0},{7,1},{8,14},{9,15},{10,... | collective-permute-start | bytes 589832 | tf_op jit(solution)/shard_map/ppermute | solution.py:186
  44.6 8.0 %copy-start.1 = (f32[512,256]{1,0:T(8,128)S(1)}, f32[512,256]{1,0:T(8,128)}, u32[]{:S(2)}) copy-start(f32[512,256]{1,0:T(8,128)} %weight.3) | copy-start | bytes 1572868
  44.6 5.7 %collective-permute-start.19 = (bf16[64,512]{1,0:T(8,128)(2,1)S(1)}, bf16[64,512]{1,0:T(8,128)(2,1)S(1)}, u32[]{:S(2)}, u32[]{:S(2)}) collective-permute-start(bf16[64,512]{1,0:T(8,128)(2,1)S(1)} %shard_map.100.refs_0_), channel_id=1, source_target_pairs={{0,8},{8,0},{16,24},{24,16},{1,9},{9,1},{17,25},{25,17},{2,10},{10... | collective-permute-start | bytes 196616 | tf_op jit(solution)/shard_map/ppermute | solution.py:186
  45.6 4.7 %collective-permute-start.20 = (bf16[64,512]{1,0:T(8,128)(2,1)S(1)}, bf16[64,512]{1,0:T(8,128)(2,1)S(1)}, u32[]{:S(2)}, u32[]{:S(2)}) collective-permute-start(bf16[64,512]{1,0:T(8,128)(2,1)S(1)} %shard_map.100.refs_0_), channel_id=1, source_target_pairs={{0,16},{8,24},{16,0},{24,8},{1,17},{9,25},{17,1},{25,9},{2,18},{10... | collective-permute-start | bytes 196616 | tf_op jit(solution)/shard_map/ppermute | solution.py:186
  47.4 5.2 %collective-permute-start.21 = (bf16[64,512]{1,0:T(8,128)(2,1)S(1)}, bf16[64,512]{1,0:T(8,128)(2,1)S(1)}, u32[]{:S(2)}, u32[]{:S(2)}) collective-permute-start(bf16[64,512]{1,0:T(8,128)(2,1)S(1)} %shard_map.100.refs_0_), channel_id=1, source_target_pairs={{0,24},{8,16},{16,8},{24,0},{1,25},{9,17},{17,9},{25,1},{2,26},{10... | collective-permute-start | bytes 196616 | tf_op jit(solution)/shard_map/ppermute | solution.py:186

commit v2 on v1

v2 whole, which is shorter than its diff:
```python
import functools
import math

import jax
import jax.numpy as jnp
import numpy as np
from jax import lax
from jax.experimental import pallas as pl
from jax.experimental.pallas import tpu as pltpu
from jax.sharding import PartitionSpec as P


BLOCK = 64
SEL = 16
CORES = 2
CHIPS = 4

MOMENTUM_DECAY = 0.9
LEARN_RATE = 0.05
HIGHEST = lax.Precision.HIGHEST
BF16, F32 = jnp.bfloat16, jnp.float32


HBM = pl.BlockSpec(memory_space=pltpu.HBM)


def vmem(count):
    return [pl.BlockSpec(memory_space=pltpu.VMEM)] * count


def dct_rows(width):
    index = np.arange(BLOCK, dtype=np.float64)
    table = np.cos(math.pi * (2.0 * index[None, :] + 1.0) * index[:, None] / (2.0 * BLOCK))
    table *= math.sqrt(2.0 / BLOCK)
    table[0] *= math.sqrt(0.5)
    return np.tile(table, (1, width // BLOCK)).astype(np.float32)


def call(kernel, outs, in_specs, flops, nbytes, scratch=(), limit=32 << 20):
    run = pl.pallas_call(
        kernel,
        out_shape=outs,
        in_specs=in_specs,
        out_specs=vmem(len(outs)),
        scratch_shapes=scratch,
        cost_estimate=pl.CostEstimate(flops=flops, bytes_accessed=nbytes, transcendentals=0),
        compiler_params=pltpu.CompilerParams(vmem_limit_bytes=limit),
    )
    return run


def dot(a, b, dims, precision=None):
    return lax.dot_general(
        a, b, (dims, ((), ())), precision=precision, preferred_element_type=F32
    )


def halves(x):
    high = x.astype(BF16)
    return high, (x - high.astype(F32)).astype(BF16)


def outer(a, b):
    (a_high, a_low), (b_high, b_low) = halves(a), halves(b)
    left = jnp.concatenate([a_high, a_low, a_high])
    return dot(left, jnp.concatenate([b_high, b_high, b_low]), ((0,), (0,)))


def position():
    member = lax.axis_index("fsdp")
    return lax.axis_index("rep"), member // CORES, lax.rem(member, CORES)


def in_hbm(x):
    return pltpu.with_memory_space_constraint(x, pltpu.HBM)


def wide(ref):
    return ref[...].astype(F32)


def start_kernel(order, rows, weight, cot, tokens, *refs):
    half, share, basis, coded_cot, own = refs[:5]
    held_order, held_rows, held_weight, held_cot, table, sems = refs[5:]
    rep, _, core = position()
    columns = weight.shape[0]
    moves = [(weight, held_weight), (order, held_order), (rows, held_rows), (cot, held_cot)]
    for k in range(own.shape[1] // columns):
        at = pl.ds(pl.multiple_of((CORES * k + core) * columns, columns), columns)
        moves.append((tokens.at[:, at], own.at[:, pl.ds(k * columns, columns)]))
    copies = [pltpu.make_async_copy(a, b, sems.at[k]) for k, (a, b) in enumerate(moves)]
    for copy in copies:
        copy.start()
    copies[0].wait()
    half[...] = held_weight[...].astype(BF16)
    part = share.shape[0]
    begin = pl.multiple_of(rep * part, part)
    share[...] = held_weight[pl.ds(begin, part), :].astype(BF16)
    copies[1].wait()
    copies[2].wait()
    for s in range(BLOCK):
        table[pl.ds(s, 1), :] = held_rows[pl.ds(held_order[s], 1), :]
    features = basis.shape[1]
    blocks = features // BLOCK
    rest = BLOCK - SEL
    for b in range(blocks):
        inside = lax.broadcasted_iota(jnp.int32, (BLOCK, features), 1) // BLOCK == b
        block = jnp.where(inside, table[...], 0.0)
        basis[pl.ds(b * SEL, SEL), :] = block[:SEL]
        basis[pl.ds(blocks * SEL + b * rest, rest), :] = block[SEL:]
    copies[3].wait()
    high, low = halves(basis[...])
    value = dot(high, held_cot[...], ((1,), (1,))) + dot(low, held_cot[...], ((1,), (1,)))
    coded_cot[...] = value.astype(BF16)
    for copy in copies[4:]:
        copy.wait()


def partial_kernel(mine, theirs, own_tok, their_tok, *outs):
    code, keep_code, own_code, far, near, keep, own_rest = outs
    _, chip, core = position()
    sent, columns = own_code.shape

    def total(mask):
        dest = chip ^ mask
        own_at = pl.ds(pl.multiple_of(dest * columns, columns), columns)
        at = pl.ds(pl.multiple_of((CORES * dest + core) * columns, columns), columns)
        value = dot(mine[...], own_tok[:, own_at], ((1,), (0,)))
        return value + dot(theirs[...], their_tok[:, at], ((1,), (0,)))

    first, last = code.at[pl.ds(0, sent), :], code.at[pl.ds(sent, sent), :]
    for mask, head, rest in (
        (1, first, near),
        (3, last, far),
        (2, keep_code, keep),
        (0, own_code, own_rest),
    ):
        value = total(mask)
        head[...] = value[:sent].astype(head.dtype)
        rest[...] = value[sent:].astype(rest.dtype)


def old_kernel(basis, momentum, kept, coded):
    sent = basis[: coded.shape[0], :]
    old = MOMENTUM_DECAY * momentum[0]
    (sent_high, sent_low), (high, low) = halves(sent), halves(old)
    code = dot(sent_high, high, ((1,), (1,))) + dot(sent_high, low, ((1,), (1,)))
    code += dot(sent_low, high, ((1,), (1,)))
    coded[...] = code
    kept[...] = old - outer(code, sent)


def join_kernel(*refs):
    at = 0
    for ref in refs[:-1]:
        refs[-1][pl.ds(at, ref.shape[0]), :] = ref[...]
        at += ref.shape[0]


def relay_kernel(keep, arrived, out):
    out[...] = (keep[...] + wide(arrived)).astype(out.dtype)


def code_kernel(keep, arrived, out):
    out[...] = (keep[...] + arrived[keep.shape[0] :, :].astype(F32)).astype(out.dtype)


def pack_kernel(scale, coded, own, arrived, late, out):
    total = own[...] + arrived[: own.shape[0], :].astype(F32) + wide(late)
    out[...] = (coded[...] + scale * total).astype(out.dtype)


def add_kernel(left, right, out):
    out[...] = (wide(left) + wide(right)).astype(out.dtype)


def moment_kernel(scale, basis, kept, own, near, late, out):
    total = own[...] + wide(near) + wide(late)
    rest = basis[basis.shape[0] - own.shape[0] :, :]
    grad = dot(total.astype(BF16), rest.astype(BF16), ((0,), (0,)))
    out[0] = kept[...] + scale * grad


def update_kernel(replicas, basis, weight, left, right, update, new_weight):
    total = wide(left) + wide(right)
    sent = basis[: total.shape[0], :]
    value = outer(total, sent) * (1.0 / replicas)
    update[...] = value
    new_weight[...] = weight[...] - LEARN_RATE * value


def input_kernel(chips, replicas, cot, *refs):
    pieces, out = refs[:-1], refs[-1]
    rep, chip, core = position()
    rows = pieces[0].shape[0]
    part = rows // replicas
    group = part * (chips - 1)
    for side in range(CORES):
        whose = lax.rem(core + side, CORES)
        own, others = pieces[2 * side : 2 * side + 2]
        begin = pl.multiple_of((CORES * chip + whose) * rows, rows)
        out[:, pl.ds(begin, rows)] = dot(cot[...], own[...], ((1,), (1,))).astype(out.dtype)
        for e in range(replicas):
            piece = others[e * group : (e + 1) * group, :]
            value = dot(cot[...], piece, ((1,), (1,))).astype(out.dtype)
            for d in range(1, chips):
                begin = (CORES * (chip ^ d) + whose) * rows + (rep ^ e) * part
                at = pl.ds(pl.multiple_of(begin, part), part)
                out[:, at] = value[:, (d - 1) * part : d * part]


def tuned(tokens, cotangent, weight, momentum, column_order):
    members, replicas = lax.axis_size("fsdp"), lax.axis_size("rep")
    chips = members // CORES
    count, width = tokens.shape
    rows, features = weight.shape
    sent = features // BLOCK * SEL
    part = rows // replicas
    shape = jax.ShapeDtypeStruct

    def permute(x, axis, target):
        pairs = [(i, target(i)) for i in range(lax.axis_size(axis))]
        return lax.ppermute(x, axis, pairs)

    def swap(x):
        return permute(x, "fsdp", lambda i: i ^ 1)

    def over_chips(x, mask):
        return permute(x, "fsdp", lambda i: i ^ (CORES * mask))

    def over_rep(x, mask):
        return permute(x, "rep", lambda i: i ^ mask)

    def simple(kernel, out, *args):
        (value,) = call(kernel, (out,), vmem(len(args)), 0, 8 * out.size)(*args)
        return value

    def join(*args):
        size = sum(x.shape[0] for x in args)
        return simple(join_kernel, shape((size, args[0].shape[1]), args[0].dtype), *args)

    their_tokens = swap(tokens)
    half, share, basis, mine, own_tokens = call(
        start_kernel,
        (
            shape((rows, features), BF16),
            shape((part, features), BF16),
            shape((features, features), F32),
            shape((features, count), BF16),
            shape((count, chips * rows), BF16),
        ),
        [HBM] * 5,
        12 * features * features * count,
        2 * count * width,
        [
            pltpu.SMEM((BLOCK,), jnp.int32),
            pltpu.VMEM((BLOCK, features), F32),
            pltpu.VMEM((rows, features), F32),
            pltpu.VMEM((count, features), BF16),
            pltpu.VMEM((BLOCK, features), F32),
            pltpu.SemaphoreType.DMA((4 + chips,)),
        ],
    )(*map(in_hbm, (column_order, jnp.asarray(dct_rows(features)), weight, cotangent, tokens)))
    theirs = swap(mine)
    shares = [over_chips(share, d) for d in range(1, chips)]

    code, rest = shape((sent, rows), BF16), shape((features - sent, rows), BF16)
    code_f32, rest_f32 = shape(code.shape, F32), shape(rest.shape, F32)
    codes, keep_code, own_code, far, near, keep, own_rest = call(
        partial_kernel,
        (shape((2 * sent, rows), BF16), code_f32, code_f32, rest, rest, rest_f32, rest_f32),
        vmem(4),
        2 * CORES * count * rows * chips * features,
        CORES * count * rows * chips * 2,
    )(mine, theirs, own_tokens, their_tokens)

    codes = over_chips(codes, 1)
    far = over_chips(far, 1)
    near = over_chips(near, 1)
    late_code = over_chips(simple(code_kernel, code, keep_code, codes), 2)
    late = over_chips(simple(relay_kernel, rest, keep, far), 2)

    kept, coded = call(
        old_kernel,
        (shape((rows, features), F32), shape((sent, rows), F32)),
        vmem(2),
        24 * rows * features * sent,
        rows * features * 8,
    )(basis, momentum)
    scale = float(count * members) ** (-0.5)
    packed = simple(functools.partial(pack_kernel, scale), code, coded, own_code, codes, late_code)
    paired = simple(add_kernel, code, packed, over_rep(packed, 1))
    update, new_weight = call(
        functools.partial(update_kernel, replicas),
        (shape(weight.shape, F32),) * 2,
        vmem(4),
        12 * rows * features * sent,
        rows * features * 12,
    )(basis, weight, paired, over_rep(paired, 2))
    (new_momentum,) = call(
        functools.partial(moment_kernel, scale),
        (shape(momentum.shape, F32),),
        vmem(5),
        2 * rows * features * features,
        rows * features * 16,
    )(basis, kept, own_rest, near, late)

    joined = join(*shares)
    spread = [over_rep(joined, e) for e in range(1, replicas)]
    gathered = join(joined, *spread)
    pieces = [half, gathered, swap(half), swap(gathered)]
    (input_grad,) = call(
        functools.partial(input_kernel, chips, replicas),
        (shape((count, width), BF16),),
        vmem(1 + len(pieces)),
        2 * count * width * features,
        2 * (count + features) * width,
    )(cotangent, *pieces)
    return input_grad, new_momentum, update, new_weight


def general(tokens, cotangent, weight, momentum, column_order):
    members, replicas = lax.axis_size("fsdp"), lax.axis_size("rep")
    features = weight.shape[1]
    whole = lax.all_gather(weight.astype(BF16), "fsdp", axis=0, tiled=True)
    input_grad = dot(cotangent, whole, ((1,), (1,))).astype(BF16)
    grad = lax.psum_scatter(
        dot(tokens, cotangent, ((0,), (0,))), "fsdp", scatter_dimension=0, tiled=True
    )
    moment = MOMENTUM_DECAY * momentum[0] + grad * float(tokens.shape[0] * members) ** (-0.5)
    lane_block = jnp.arange(features) // BLOCK
    chosen = jnp.asarray(dct_rows(features))[column_order[:SEL]]
    basis = jnp.concatenate(
        [jnp.where(lane_block == b, chosen, 0.0) for b in range(features // BLOCK)]
    )
    coded = dot(moment, basis, ((1,), (1,)), HIGHEST)
    new_momentum = (moment - dot(coded, basis, ((1,), (0,)), HIGHEST))[None]
    summed = jnp.sum(lax.all_gather(coded, "rep", axis=0), axis=0)
    update = dot(summed, basis, ((1,), (0,)), HIGHEST) / replicas
    return input_grad, new_momentum, update, weight - LEARN_RATE * update


def solution(mesh):
    in_specs = (
        P(("rep", "fsdp"), None),
        P(("rep", "fsdp"), None),
        P("fsdp", None),
        P("rep", "fsdp", None),
        P(),
    )
    out_specs = (P(("rep", "fsdp"), None), P("rep", "fsdp", None), P("fsdp", None), P("fsdp", None))
    members, replicas = mesh.shape["fsdp"], mesh.shape["rep"]
    line = members == CHIPS * CORES and replicas == CHIPS

    def on_device(*args):
        if not line:
            return general(*args)
        return tuned(*args)

    return jax.shard_map(
        on_device, mesh=mesh, in_specs=in_specs, out_specs=out_specs, check_vma=False
    )
```

time: 55.6 us -> 55.8 us (level)
  waiting for transfers between devices: 17.9 us -> 27.6 us
  local copies, waits for them, and re-layouts: 4.85 us -> 0.02 us
  starting transfers between devices: 24 us -> 19.9 us
    ppermute x22 -> x17, waiting for transfers between devices: 17.9 us -> 27.6 us  [permute(): return lax.ppermute(x, axis, pairs)]
    unnamed x16 -> x6, local copies, waits for them, and re-layouts: 4.85 us -> 0.02 us
    ppermute x22 -> x17, starting transfers between devices: 24 us -> 19.9 us  [permute(): return lax.ppermute(x, axis, pairs)]
    pallas_call x1, Pallas kernels: 1.23 us -> 0.66 us  [tuned(): call(old_kernel, (shape((rows, features), F32), shape((sent, rows), F32))...]
    pallas_call x5 -> x8, Pallas kernels: 2.9 us -> 2.96 us  [the longest x1 2.1 us: tuned(): call(functools.partial(input_kernel, chips, replicas), (shape((count, wid...]
  transfers between devices with their start and end apart: 22 -> 17, of which waited for: 9 -> 10; matrix products, arithmetic and copies ran while one was open for 0% -> 0% of each run, Pallas kernels for 12% -> 12%
where the time goes in v2:
time: 55.8 us; the launch traced here: 55.6 us
  waiting for transfers between devices  27.6 us (49%)
  starting transfers between devices  19.9 us (36%)
  Pallas kernels  7.49 us (13%)
  between operations  0.72 us (1%)
    ppermute x17, waiting for transfers between devices, permute(): return lax.ppermute(x, axis, pairs)  27.6 us
    ppermute x17, starting transfers between devices, permute(): return lax.ppermute(x, axis, pairs)  19.9 us
    pallas_call x1, Pallas kernels, tuned(): call(functools.partial(input_kernel, chips, replicas), (shape((count, wid...  2.1 us
    pallas_call x1, Pallas kernels, tuned(): call(start_kernel, (shape((rows, features), BF16), shape((part, features)...  1.53 us
    pallas_call x1, Pallas kernels, tuned(): call(functools.partial(update_kernel, replicas), (shape(weight.shape, F32...  1.25 us
  transfers between devices with their start and end apart: 17, of which 10 were waited for; matrix products, arithmetic and copies ran while one was open for 0% of the time, Pallas kernels for 12%

profile of v2, /device:TPU:0, one launch (start us, length us, event | category | flops | bytes accessed | tf_op | source)
XLA Modules:
  0.0 55.6 jit_solution(16503653628485744038)
XLA Ops:
  0.6 0.6 %collective-permute-start.9 = (bf16[192,4096]{1,0:T(8,128)(2,1)}, bf16[192,4096]{1,0:T(8,128)(2,1)S(1)}, u32[]{:S(2)}, u32[]{:S(2)}) collective-permute-start(bf16[192,4096]{1,0:T(8,128)(2,1)} %tokens.1), channel_id=1, source_target_pairs={{0,1},{1,0},{2,3},{3,2},{4,5},{5,4},{6,7},{7,6},{8,9},{9,8},{10,11... | collective-permute-start | bytes 4718600 | tf_op jit(solution)/shard_map/ppermute | solution.py:223
  1.2 1.5 %shard_map.93 = (bf16[512,256]{1,0:T(8,128)(2,1)S(1)}, bf16[128,256]{1,0:T(8,128)(2,1)S(1)}, f32[256,256]{1,0:T(8,128)S(1)}, bf16[256,192]{1,0:T(8,128)(2,1)S(1)}, bf16[192,2048]{1,0:T(8,128)(2,1)S(1)}) custom-call(s32[64]{0:T(128)} %order.1, f32[64,256]{1,0:T(8,128)} %constant.2.clone.rows, f32[512,256]{1,0:T(8,128)} %weight.3, bf16[192,256]{1,0:T(8,128)(2,1)} %cot.3, ...), custom_call_target="tpu_custom_call" | custom-call | flops 150994944 | bytes 1572864 | tf_op jit(solution)/shard_map/pallas_call | solution.py:243
  2.7 2.6 %collective-permute-start = (bf16[128,256]{1,0:T(8,128)(2,1)S(1)}, bf16[128,256]{1,0:T(8,128)(2,1)S(1)}, u32[]{:S(2)}, u32[]{:S(2)}) collective-permute-start(bf16[128,256]{1,0:T(8,128)(2,1)S(1)} %get-tuple-element.21), channel_id=1, source_target_pairs={{0,2},{1,3},{2,0},{3,1},{4,6},{5,7},{6,4},{7,5},{8,10},{9,11},{10,... | collective-permute-start | bytes 196616 | tf_op jit(solution)/shard_map/ppermute | solution.py:223
  5.4 2.6 %collective-permute-start.1 = (bf16[128,256]{1,0:T(8,128)(2,1)S(1)}, bf16[128,256]{1,0:T(8,128)(2,1)S(1)}, u32[]{:S(2)}, u32[]{:S(2)}) collective-permute-start(bf16[128,256]{1,0:T(8,128)(2,1)S(1)} %get-tuple-element.21), channel_id=1, source_target_pairs={{0,4},{1,5},{2,6},{3,7},{4,0},{5,1},{6,2},{7,3},{8,12},{9,13},{10,... | collective-permute-start | bytes 196616 | tf_op jit(solution)/shard_map/ppermute | solution.py:223
  8.0 0.0 collective-permute-start.2
  8.0 0.2 collective-permute-done.refs_0_
  8.1 4.3 %collective-permute-done.1.refs_1_ = bf16[128,256]{1,0:T(8,128)(2,1)S(1)} collective-permute-done((bf16[128,256]{1,0:T(8,128)(2,1)S(1)}, bf16[128,256]{1,0:T(8,128)(2,1)S(1)}, u32[]{:S(2)}, u32[]{:S(2)}) %collective-permute-start.1) | collective-permute-done | bytes 65568 | tf_op jit(solution)/shard_map/ppermute | solution.py:223
  12.4 1.6 %collective-permute-done.2.refs_2_ = bf16[128,256]{1,0:T(8,128)(2,1)S(1)} collective-permute-done((bf16[128,256]{1,0:T(8,128)(2,1)S(1)}, bf16[128,256]{1,0:T(8,128)(2,1)S(1)}, u32[]{:S(2)}, u32[]{:S(2)}) %collective-permute-start.2) | collective-permute-done | bytes 65568 | tf_op jit(solution)/shard_map/ppermute | solution.py:223
  14.0 1.6 %collective-permute-start.3 = (bf16[384,256]{1,0:T(8,128)(2,1)S(1)}, bf16[384,256]{1,0:T(8,128)(2,1)S(1)}, u32[]{:S(2)}, u32[]{:S(2)}) collective-permute-start(bf16[384,256]{1,0:T(8,128)(2,1)S(1)} %shard_map.94.refs_0_), channel_id=1, source_target_pairs={{0,8},{8,0},{16,24},{24,16},{1,9},{9,1},{17,25},{25,17},{2,10},{10... | collective-permute-start | bytes 589832 | tf_op jit(solution)/shard_map/ppermute | solution.py:223
  15.6 1.5 %collective-permute-start.4 = (bf16[384,256]{1,0:T(8,128)(2,1)S(1)}, bf16[384,256]{1,0:T(8,128)(2,1)S(1)}, u32[]{:S(2)}, u32[]{:S(2)}) collective-permute-start(bf16[384,256]{1,0:T(8,128)(2,1)S(1)} %shard_map.94.refs_0_), channel_id=1, source_target_pairs={{0,16},{8,24},{16,0},{24,8},{1,17},{9,25},{17,1},{25,9},{2,18},{10... | collective-permute-start | bytes 589832 | tf_op jit(solution)/shard_map/ppermute | solution.py:223
  17.1 0.5 collective-permute-start.5
  17.6 4.0 %collective-permute-done.3.refs_1_ = bf16[384,256]{1,0:T(8,128)(2,1)S(1)} collective-permute-done((bf16[384,256]{1,0:T(8,128)(2,1)S(1)}, bf16[384,256]{1,0:T(8,128)(2,1)S(1)}, u32[]{:S(2)}, u32[]{:S(2)}) %collective-permute-start.3) | collective-permute-done | bytes 196640 | tf_op jit(solution)/shard_map/ppermute | solution.py:223
  21.6 3.8 %collective-permute-done.4.refs_2_ = bf16[384,256]{1,0:T(8,128)(2,1)S(1)} collective-permute-done((bf16[384,256]{1,0:T(8,128)(2,1)S(1)}, bf16[384,256]{1,0:T(8,128)(2,1)S(1)}, u32[]{:S(2)}, u32[]{:S(2)}) %collective-permute-start.4) | collective-permute-done | bytes 196640 | tf_op jit(solution)/shard_map/ppermute | solution.py:223
  25.4 0.0 collective-permute-done.5.refs_3_
  25.4 0.1 shard_map.95.refs_1_
  25.4 0.1 collective-permute-start.7
  25.5 0.5 collective-permute-start.8
  26.0 2.0 %collective-permute-done.8.theirs = bf16[256,192]{1,0:T(8,128)(2,1)S(1)} collective-permute-done((bf16[256,192]{1,0:T(8,128)(2,1)S(1)}, bf16[256,192]{1,0:T(8,128)(2,1)S(1)}, u32[]{:S(2)}, u32[]{:S(2)}) %collective-permute-start.8) | collective-permute-done | bytes 98336 | tf_op jit(solution)/shard_map/ppermute | solution.py:223
  28.0 0.0 collective-permute-done.9.their_tok
  28.0 0.0 copy-start.1
  28.0 0.7 %shard_map.98 = (bf16[128,512]{1,0:T(8,128)(2,1)S(1)}, f32[64,512]{1,0:T(8,128)S(1)}, f32[64,512]{1,0:T(8,128)S(1)}, bf16[192,512]{1,0:T(8,128)(2,1)S(1)}, bf16[...) custom-call(bf16[256,192]{1,0:T(8,128)(2,1)S(1)} %get-tuple-element.24.mine, ...), custom_call_target="tpu_custom_call" | custom-call | flops 402653184 | bytes 1572864 | tf_op jit(solution)/shard_map/pallas_call | solution.py:269
  28.7 0.0 copy-start.2
  28.7 2.0 %collective-permute-start.11 = (bf16[192,512]{1,0:T(8,128)(2,1)S(1)}, bf16[192,512]{1,0:T(8,128)(2,1)S(1)}, u32[]{:S(2)}, u32[]{:S(2)}) collective-permute-start(bf16[192,512]{1,0:T(8,128)(2,1)S(1)} %get-tuple-element.29), channel_id=1, source_target_pairs={{0,2},{1,3},{2,0},{3,1},{4,6},{5,7},{6,4},{7,5},{8,10},{9,11},{10,... | collective-permute-start | bytes 589832 | tf_op jit(solution)/shard_map/ppermute | solution.py:223
  30.7 0.1 collective-permute-start.13
  30.8 0.0 collective-permute-start.6
  30.8 7.9 %collective-permute-done.13.arrived = bf16[128,512]{1,0:T(8,128)(2,1)S(1)} collective-permute-done((bf16[128,512]{1,0:T(8,128)(2,1)S(1)}, bf16[128,512]{1,0:T(8,128)(2,1)S(1)}, u32[]{:S(2)}, u32[]{:S(2)}) %collective-permute-start.13) | collective-permute-done | bytes 131104 | tf_op jit(solution)/shard_map/ppermute | solution.py:223
  38.7 2.2 %collective-permute-start.14 = (bf16[64,512]{1,0:T(8,128)(2,1)S(1)}, bf16[64,512]{1,0:T(8,128)(2,1)S(1)}, u32[]{:S(2)}, u32[]{:S(2)}) collective-permute-start(bf16[64,512]{1,0:T(8,128)(2,1)S(1)} %shard_map.101), channel_id=1, source_target_pairs={{0,4},{1,5},{2,6},{3,7},{4,0},{5,1},{6,2},{7,3},{8,12},{9,13},{10,... | collective-permute-start | bytes 196616 | tf_op jit(solution)/shard_map/ppermute | solution.py:223
  40.9 0.3 collective-permute-start.10
  41.2 0.0 collective-permute-done.11.arrived
  41.3 2.3 %collective-permute-start.12 = (bf16[192,512]{1,0:T(8,128)(2,1)S(1)}, bf16[192,512]{1,0:T(8,128)(2,1)S(1)}, u32[]{:S(2)}, u32[]{:S(2)}) collective-permute-start(bf16[192,512]{1,0:T(8,128)(2,1)S(1)} %shard_map.99), channel_id=1, source_target_pairs={{0,4},{1,5},{2,6},{3,7},{4,0},{5,1},{6,2},{7,3},{8,12},{9,13},{10,... | collective-permute-start | bytes 589832 | tf_op jit(solution)/shard_map/ppermute | solution.py:223
  43.6 0.0 copy-done.1
  43.6 0.7 %shard_map.97 = (f32[512,256]{1,0:T(8,128)S(1)}, f32[64,512]{1,0:T(8,128)S(1)}) custom-call(f32[256,256]{1,0:T(8,128)S(1)} %get-tuple-element.22.basis, f32[1,512,256]{2,1,0:T(8,128)S(1)} %copy-done.1), custom_call_target="tpu_custom_call" | custom-call | flops 201326592 | bytes 1048576 | tf_op jit(solution)/shard_map/pallas_call | solution.py:283
  44.2 0.3 collective-permute-done.14.late
  44.6 1.4 %collective-permute-start.15 = (bf16[64,512]{1,0:T(8,128)(2,1)S(1)}, bf16[64,512]{1,0:T(8,128)(2,1)S(1)}, u32[]{:S(2)}, u32[]{:S(2)}) collective-permute-start(bf16[64,512]{1,0:T(8,128)(2,1)S(1)} %shard_map.102.left), channel_id=1, source_target_pairs={{0,8},{8,0},{16,24},{24,16},{1,9},{9,1},{17,25},{25,17},{2,10},{10... | collective-permute-start | bytes 196616 | tf_op jit(solution)/shard_map/ppermute | solution.py:223
  46.0 2.9 %collective-permute-done.15.right = bf16[64,512]{1,0:T(8,128)(2,1)S(1)} collective-permute-done((bf16[64,512]{1,0:T(8,128)(2,1)S(1)}, bf16[64,512]{1,0:T(8,128)(2,1)S(1)}, u32[]{:S(2)}, u32[]{:S(2)}) %collective-permute-start.15) | collective-permute-done | bytes 65568 | tf_op jit(solution)/shard_map/ppermute | solution.py:223
  48.9 0.0 copy-start
  49.0 1.6 %collective-permute-start.16 = (bf16[64,512]{1,0:T(8,128)(2,1)S(1)}, bf16[64,512]{1,0:T(8,128)(2,1)S(1)}, u32[]{:S(2)}, u32[]{:S(2)}) collective-permute-start(bf16[64,512]{1,0:T(8,128)(2,1)S(1)} %shard_map.103.left), channel_id=1, source_target_pairs={{0,16},{8,24},{16,0},{24,8},{1,17},{9,25},{17,1},{25,9},{2,18},{10... | collective-permute-start | bytes 196616 | tf_op jit(solution)/shard_map/ppermute | solution.py:223
  50.6 0.0 collective-permute-done.6.refs_2_
  50.6 0.0 collective-permute-done.7.refs_3_
  50.6 0.0 copy-done.2
  50.6 2.1 %shard_map.96 = bf16[192,4096]{1,0:T(8,128)(2,1)} custom-call(bf16[192,256]{1,0:T(8,128)(2,1)S(1)} %copy-done.2, bf16[512,256]{1,0:T(8,128)(2,1)S(1)} %get-tuple-element.20.refs_0_, bf16[1536,256]{1,0:T(8,128)(2,1)S(1)} %shard_map.95.refs_1_, bf16[512,256]{1,0:T(8,128)(2,1)S(1)} %collective-permute-done.6.refs_2_, ...), custom_call_target="tpu_custom_call" | custom-call | flops 402653184 | bytes 3670016 | tf_op jit(solution)/shard_map/pallas_call | solution.py:312
  52.7 0.6 %collective-permute-done.16.right = bf16[64,512]{1,0:T(8,128)(2,1)S(1)} collective-permute-done((bf16[64,512]{1,0:T(8,128)(2,1)S(1)}, bf16[64,512]{1,0:T(8,128)(2,1)S(1)}, u32[]{:S(2)}, u32[]{:S(2)}) %collective-permute-start.16) | collective-permute-done | bytes 65568 | tf_op jit(solution)/shard_map/ppermute | solution.py:223
  53.3 0.0 copy-done
  53.3 1.2 %shard_map.104 = (f32[512,256]{1,0:T(8,128)}, f32[512,256]{1,0:T(8,128)}) custom-call(f32[256,256]{1,0:T(8,128)S(1)} %get-tuple-element.22.basis, f32[512,256]{1,0:T(8,128)S(1)} %copy-done, bf16[64,512]{1,0:T(8,128)(2,1)S(1)} %shard_map.103.left, bf16[64,512]{1,0:T(8,128)(2,1)S(1)} %collective-permute-done.16.right), custom_call_target="tpu_custom_call" | custom-call | flops 100663296 | bytes 1572864 | tf_op jit(solution)/shard_map/pallas_call | solution.py:293
  54.5 0.0 collective-permute-done.10.near
  54.5 0.0 collective-permute-done.12.late
  54.5 1.1 %shard_map.100 = f32[1,512,256]{2,1,0:T(8,128)} custom-call(f32[256,256]{1,0:T(8,128)S(1)} %get-tuple-element.22.basis, f32[512,256]{1,0:T(8,128)S(1)} %get-tuple-element.23.kept, f32[192,512]{1,0:T(8,128)S(1)} %get-tuple-element.26.own, bf16[192,512]{1,0:T(8,128)(2,1)S(1)} %collective-permute-done.10.near, bf16[192,512]{1,0:T(8,128)(2,1)S(1)} %collective-permute-done.12.late), custom_call_target="tpu_custom_call" | custom-call | flops 67108864 | bytes 2097152 | tf_op jit(solution)/shard_map/pallas_call | solution.py:300
  (5 shorter events, 0.1 us)
Async XLA Ops:
  0.6 27.3 %collective-permute-start.9 = (bf16[192,4096]{1,0:T(8,128)(2,1)}, bf16[192,4096]{1,0:T(8,128)(2,1)S(1)}, u32[]{:S(2)}, u32[]{:S(2)}) collective-permute-start(bf16[192,4096]{1,0:T(8,128)(2,1)} %tokens.1), channel_id=1, source_target_pairs={{0,1},{1,0},{2,3},{3,2},{4,5},{5,4},{6,7},{7,6},{8,9},{9,8},{10,11... | collective-permute-start | bytes 4718600 | tf_op jit(solution)/shard_map/ppermute | solution.py:223
  2.7 5.4 %collective-permute-start = (bf16[128,256]{1,0:T(8,128)(2,1)S(1)}, bf16[128,256]{1,0:T(8,128)(2,1)S(1)}, u32[]{:S(2)}, u32[]{:S(2)}) collective-permute-start(bf16[128,256]{1,0:T(8,128)(2,1)S(1)} %get-tuple-element.21), channel_id=1, source_target_pairs={{0,2},{1,3},{2,0},{3,1},{4,6},{5,7},{6,4},{7,5},{8,10},{9,11},{10,... | collective-permute-start | bytes 196616 | tf_op jit(solution)/shard_map/ppermute | solution.py:223
  5.4 7.0 %collective-permute-start.1 = (bf16[128,256]{1,0:T(8,128)(2,1)S(1)}, bf16[128,256]{1,0:T(8,128)(2,1)S(1)}, u32[]{:S(2)}, u32[]{:S(2)}) collective-permute-start(bf16[128,256]{1,0:T(8,128)(2,1)S(1)} %get-tuple-element.21), channel_id=1, source_target_pairs={{0,4},{1,5},{2,6},{3,7},{4,0},{5,1},{6,2},{7,3},{8,12},{9,13},{10,... | collective-permute-start | bytes 196616 | tf_op jit(solution)/shard_map/ppermute | solution.py:223
  8.0 6.1 %collective-permute-start.2 = (bf16[128,256]{1,0:T(8,128)(2,1)S(1)}, bf16[128,256]{1,0:T(8,128)(2,1)S(1)}, u32[]{:S(2)}, u32[]{:S(2)}) collective-permute-start(bf16[128,256]{1,0:T(8,128)(2,1)S(1)} %get-tuple-element.21), channel_id=1, source_target_pairs={{0,6},{1,7},{2,4},{3,5},{4,2},{5,3},{6,0},{7,1},{8,14},{9,15},{10,... | collective-permute-start | bytes 196616 | tf_op jit(solution)/shard_map/ppermute | solution.py:223
  14.0 7.6 %collective-permute-start.3 = (bf16[384,256]{1,0:T(8,128)(2,1)S(1)}, bf16[384,256]{1,0:T(8,128)(2,1)S(1)}, u32[]{:S(2)}, u32[]{:S(2)}) collective-permute-start(bf16[384,256]{1,0:T(8,128)(2,1)S(1)} %shard_map.94.refs_0_), channel_id=1, source_target_pairs={{0,8},{8,0},{16,24},{24,16},{1,9},{9,1},{17,25},{25,17},{2,10},{10... | collective-permute-start | bytes 589832 | tf_op jit(solution)/shard_map/ppermute | solution.py:223
  15.6 9.8 %collective-permute-start.4 = (bf16[384,256]{1,0:T(8,128)(2,1)S(1)}, bf16[384,256]{1,0:T(8,128)(2,1)S(1)}, u32[]{:S(2)}, u32[]{:S(2)}) collective-permute-start(bf16[384,256]{1,0:T(8,128)(2,1)S(1)} %shard_map.94.refs_0_), channel_id=1, source_target_pairs={{0,16},{8,24},{16,0},{24,8},{1,17},{9,25},{17,1},{25,9},{2,18},{10... | collective-permute-start | bytes 589832 | tf_op jit(solution)/shard_map/ppermute | solution.py:223
  17.1 8.3 %collective-permute-start.5 = (bf16[384,256]{1,0:T(8,128)(2,1)S(1)}, bf16[384,256]{1,0:T(8,128)(2,1)S(1)}, u32[]{:S(2)}, u32[]{:S(2)}) collective-permute-start(bf16[384,256]{1,0:T(8,128)(2,1)S(1)} %shard_map.94.refs_0_), channel_id=1, source_target_pairs={{0,24},{8,16},{16,8},{24,0},{1,25},{9,17},{17,9},{25,1},{2,26},{10... | collective-permute-start | bytes 589832 | tf_op jit(solution)/shard_map/ppermute | solution.py:223
  25.4 25.2 %collective-permute-start.7 = (bf16[1536,256]{1,0:T(8,128)(2,1)S(1)}, bf16[1536,256]{1,0:T(8,128)(2,1)S(1)}, u32[]{:S(2)}, u32[]{:S(2)}) collective-permute-start(bf16[1536,256]{1,0:T(8,128)(2,1)S(1)} %shard_map.95.refs_1_), channel_id=1, source_target_pairs={{0,1},{1,0},{2,3},{3,2},{4,5},{5,4},{6,7},{7,6},{8,9},{9,8},{10,11... | collective-permute-start | bytes 2359304 | tf_op jit(solution)/shard_map/ppermute | solution.py:223
  25.5 2.5 %collective-permute-start.8 = (bf16[256,192]{1,0:T(8,128)(2,1)S(1)}, bf16[256,192]{1,0:T(8,128)(2,1)S(1)}, u32[]{:S(2)}, u32[]{:S(2)}) collective-permute-start(bf16[256,192]{1,0:T(8,128)(2,1)S(1)} %get-tuple-element.24.mine), channel_id=1, source_target_pairs={{0,1},{1,0},{2,3},{3,2},{4,5},{5,4},{6,7},{7,6},{8,9},{9,8},{10,11... | collective-permute-start | bytes 294920 | tf_op jit(solution)/shard_map/ppermute | solution.py:223
  28.0 15.6 %copy-start.1 = (f32[1,512,256]{2,1,0:T(8,128)S(1)}, f32[1,512,256]{2,1,0:T(8,128)}, u32[]{:S(2)}) copy-start(f32[1,512,256]{2,1,0:T(8,128)} %momentum.1) | copy-start | bytes 1572868
  28.7 21.9 %copy-start.2 = (bf16[192,256]{1,0:T(8,128)(2,1)S(1)}, bf16[192,256]{1,0:T(8,128)(2,1)}, u32[]{:S(2)}) copy-start(bf16[192,256]{1,0:T(8,128)(2,1)} %cot.3) | copy-start | bytes 294916
  28.7 12.5 %collective-permute-start.11 = (bf16[192,512]{1,0:T(8,128)(2,1)S(1)}, bf16[192,512]{1,0:T(8,128)(2,1)S(1)}, u32[]{:S(2)}, u32[]{:S(2)}) collective-permute-start(bf16[192,512]{1,0:T(8,128)(2,1)S(1)} %get-tuple-element.29), channel_id=1, source_target_pairs={{0,2},{1,3},{2,0},{3,1},{4,6},{5,7},{6,4},{7,5},{8,10},{9,11},{10,... | collective-permute-start | bytes 589832 | tf_op jit(solution)/shard_map/ppermute | solution.py:223
  30.7 8.0 %collective-permute-start.13 = (bf16[128,512]{1,0:T(8,128)(2,1)S(1)}, bf16[128,512]{1,0:T(8,128)(2,1)S(1)}, u32[]{:S(2)}, u32[]{:S(2)}) collective-permute-start(bf16[128,512]{1,0:T(8,128)(2,1)S(1)} %get-tuple-element.32), channel_id=1, source_target_pairs={{0,2},{1,3},{2,0},{3,1},{4,6},{5,7},{6,4},{7,5},{8,10},{9,11},{10,... | collective-permute-start | bytes 393224 | tf_op jit(solution)/shard_map/ppermute | solution.py:223
  30.8 19.8 %collective-permute-start.6 = (bf16[512,256]{1,0:T(8,128)(2,1)S(1)}, bf16[512,256]{1,0:T(8,128)(2,1)S(1)}, u32[]{:S(2)}, u32[]{:S(2)}) collective-permute-start(bf16[512,256]{1,0:T(8,128)(2,1)S(1)} %get-tuple-element.20.refs_0_), channel_id=1, source_target_pairs={{0,1},{1,0},{2,3},{3,2},{4,5},{5,4},{6,7},{7,6},{8,9},{9,8},{10,11... | collective-permute-start | bytes 786440 | tf_op jit(solution)/shard_map/ppermute | solution.py:223
  38.7 5.8 %collective-permute-start.14 = (bf16[64,512]{1,0:T(8,128)(2,1)S(1)}, bf16[64,512]{1,0:T(8,128)(2,1)S(1)}, u32[]{:S(2)}, u32[]{:S(2)}) collective-permute-start(bf16[64,512]{1,0:T(8,128)(2,1)S(1)} %shard_map.101), channel_id=1, source_target_pairs={{0,4},{1,5},{2,6},{3,7},{4,0},{5,1},{6,2},{7,3},{8,12},{9,13},{10,... | collective-permute-start | bytes 196616 | tf_op jit(solution)/shard_map/ppermute | solution.py:223
  40.9 13.6 %collective-permute-start.10 = (bf16[192,512]{1,0:T(8,128)(2,1)S(1)}, bf16[192,512]{1,0:T(8,128)(2,1)S(1)}, u32[]{:S(2)}, u32[]{:S(2)}) collective-permute-start(bf16[192,512]{1,0:T(8,128)(2,1)S(1)} %get-tuple-element.27), channel_id=1, source_target_pairs={{0,2},{1,3},{2,0},{3,1},{4,6},{5,7},{6,4},{7,5},{8,10},{9,11},{10,... | collective-permute-start | bytes 589832 | tf_op jit(solution)/shard_map/ppermute | solution.py:223
  41.3 13.3 %collective-permute-start.12 = (bf16[192,512]{1,0:T(8,128)(2,1)S(1)}, bf16[192,512]{1,0:T(8,128)(2,1)S(1)}, u32[]{:S(2)}, u32[]{:S(2)}) collective-permute-start(bf16[192,512]{1,0:T(8,128)(2,1)S(1)} %shard_map.99), channel_id=1, source_target_pairs={{0,4},{1,5},{2,6},{3,7},{4,0},{5,1},{6,2},{7,3},{8,12},{9,13},{10,... | collective-permute-start | bytes 589832 | tf_op jit(solution)/shard_map/ppermute | solution.py:223
  44.6 4.3 %collective-permute-start.15 = (bf16[64,512]{1,0:T(8,128)(2,1)S(1)}, bf16[64,512]{1,0:T(8,128)(2,1)S(1)}, u32[]{:S(2)}, u32[]{:S(2)}) collective-permute-start(bf16[64,512]{1,0:T(8,128)(2,1)S(1)} %shard_map.102.left), channel_id=1, source_target_pairs={{0,8},{8,0},{16,24},{24,16},{1,9},{9,1},{17,25},{25,17},{2,10},{10... | collective-permute-start | bytes 196616 | tf_op jit(solution)/shard_map/ppermute | solution.py:223
  48.9 4.3 %copy-start = (f32[512,256]{1,0:T(8,128)S(1)}, f32[512,256]{1,0:T(8,128)}, u32[]{:S(2)}) copy-start(f32[512,256]{1,0:T(8,128)} %weight.3) | copy-start | bytes 1572868
  49.0 4.3 %collective-permute-start.16 = (bf16[64,512]{1,0:T(8,128)(2,1)S(1)}, bf16[64,512]{1,0:T(8,128)(2,1)S(1)}, u32[]{:S(2)}, u32[]{:S(2)}) collective-permute-start(bf16[64,512]{1,0:T(8,128)(2,1)S(1)} %shard_map.103.left), channel_id=1, source_target_pairs={{0,16},{8,24},{16,0},{24,8},{1,17},{9,25},{17,1},{25,9},{2,18},{10... | collective-permute-start | bytes 196616 | tf_op jit(solution)/shard_map/ppermute | solution.py:223

commit v3 on v2

--- a/solution.py
+++ b/solution.py
@@ -14,6 +14,7 @@
 SEL = 16
 CORES = 2
 CHIPS = 4
+ARRIVAL = (1, 2, 3)
 
 MOMENTUM_DECAY = 0.9
 LEARN_RATE = 0.05
@@ -36,15 +37,16 @@
     return np.tile(table, (1, width // BLOCK)).astype(np.float32)
 
 
-def call(kernel, outs, in_specs, flops, nbytes, scratch=(), limit=32 << 20):
+def call(kernel, outs, in_specs, flops, nbytes, scratch=(), out_spec=None, aliases=None):
     run = pl.pallas_call(
         kernel,
         out_shape=outs,
         in_specs=in_specs,
-        out_specs=vmem(len(outs)),
+        out_specs=[out_spec or pl.BlockSpec(memory_space=pltpu.VMEM)] * len(outs),
+        input_output_aliases=aliases or {},
         scratch_shapes=scratch,
         cost_estimate=pl.CostEstimate(flops=flops, bytes_accessed=nbytes, transcendentals=0),
-        compiler_params=pltpu.CompilerParams(vmem_limit_bytes=limit),
+        compiler_params=pltpu.CompilerParams(vmem_limit_bytes=32 << 20),
     )
     return run
 
@@ -174,39 +176,67 @@
     out[...] = (wide(left) + wide(right)).astype(out.dtype)
 
 
-def moment_kernel(scale, basis, kept, own, near, late, out):
+def final_kernel(scale, replicas, basis, kept, own, near, late, weight, left, right, *refs):
+    (moment, update, new_weight), (stage, sems) = refs[:3], refs[3:]
     total = own[...] + wide(near) + wide(late)
     rest = basis[basis.shape[0] - own.shape[0] :, :]
     grad = dot(total.astype(BF16), rest.astype(BF16), ((0,), (0,)))
-    out[0] = kept[...] + scale * grad
-
-
-def update_kernel(replicas, basis, weight, left, right, update, new_weight):
-    total = wide(left) + wide(right)
-    sent = basis[: total.shape[0], :]
-    value = outer(total, sent) * (1.0 / replicas)
-    update[...] = value
-    new_weight[...] = weight[...] - LEARN_RATE * value
-
-
-def input_kernel(chips, replicas, cot, *refs):
-    pieces, out = refs[:-1], refs[-1]
+    stage[0] = kept[...] + scale * grad
+    copies = [
+        pltpu.make_async_copy(stage.at[0], moment.at[0], sems.at[0]),
+        pltpu.make_async_copy(stage.at[1], update, sems.at[1]),
+        pltpu.make_async_copy(stage.at[2], new_weight, sems.at[2]),
+    ]
+    copies[0].start()
+    code = wide(left) + wide(right)
+    value = outer(code, basis[: code.shape[0], :]) * (1.0 / replicas)
+    stage[1] = value
+    copies[1].start()
+    stage[2] = weight[...] - LEARN_RATE * value
+    copies[2].start()
+    for copy in copies:
+        copy.wait()
+
+
+def send_blocks(cot, piece, blocks, stage, out, sems, done):
+    start = sum(size for _, size in done)
+    stage[:, pl.ds(start, piece.shape[0])] = dot(cot[...], piece, ((1,), (1,))).astype(stage.dtype)
+    for begin, size in blocks:
+        to = out.at[:, pl.ds(pl.multiple_of(begin, size), size)]
+        copy = pltpu.make_async_copy(stage.at[:, pl.ds(start, size)], to, sems.at[len(done)])
+        copy.start()
+        done.append((copy, size))
+        start += size
+
+
+def places(rows, replicas, side, e):
     rep, chip, core = position()
-    rows = pieces[0].shape[0]
     part = rows // replicas
-    group = part * (chips - 1)
-    for side in range(CORES):
-        whose = lax.rem(core + side, CORES)
-        own, others = pieces[2 * side : 2 * side + 2]
-        begin = pl.multiple_of((CORES * chip + whose) * rows, rows)
-        out[:, pl.ds(begin, rows)] = dot(cot[...], own[...], ((1,), (1,))).astype(out.dtype)
-        for e in range(replicas):
-            piece = others[e * group : (e + 1) * group, :]
-            value = dot(cot[...], piece, ((1,), (1,))).astype(out.dtype)
-            for d in range(1, chips):
-                begin = (CORES * (chip ^ d) + whose) * rows + (rep ^ e) * part
-                at = pl.ds(pl.multiple_of(begin, part), part)
-                out[:, at] = value[:, (d - 1) * part : d * part]
+    whose = lax.rem(core + side, CORES)
+    return [((CORES * (chip ^ d) + whose) * rows + (rep ^ e) * part, part) for d in ARRIVAL]
+
+
+def early_kernel(replicas, rows, cot, mine, theirs, out, stage, sems):
+    _, chip, core = position()
+    done = []
+    for side, piece in enumerate((mine, theirs)):
+        begin = (CORES * chip + lax.rem(core + side, CORES)) * rows
+        blocks = places(rows, replicas, side, 0)
+        send_blocks(cot, piece[:rows, :], [(begin, rows)], stage, out, sems, done)
+        send_blocks(cot, piece[rows:, :], blocks, stage, out, sems, done)
+    for copy, _ in done:
+        copy.wait()
+
+
+def later_kernel(replicas, rows, _, cot, mine, theirs, out, stage, sems):
+    done = []
+    group = rows // replicas * len(ARRIVAL)
+    for side, piece in enumerate((mine, theirs)):
+        for e in range(1, replicas):
+            block = piece[(e - 1) * group : e * group, :]
+            send_blocks(cot, block, places(rows, replicas, side, e), stage, out, sems, done)
+    for copy, _ in done:
+        copy.wait()
 
 
 def tuned(tokens, cotangent, weight, momentum, column_order):
@@ -290,32 +320,39 @@
     scale = float(count * members) ** (-0.5)
     packed = simple(functools.partial(pack_kernel, scale), code, coded, own_code, codes, late_code)
     paired = simple(add_kernel, code, packed, over_rep(packed, 1))
-    update, new_weight = call(
-        functools.partial(update_kernel, replicas),
-        (shape(weight.shape, F32),) * 2,
-        vmem(4),
-        12 * rows * features * sent,
-        rows * features * 12,
-    )(basis, weight, paired, over_rep(paired, 2))
-    (new_momentum,) = call(
-        functools.partial(moment_kernel, scale),
-        (shape(momentum.shape, F32),),
-        vmem(5),
+    new_momentum, update, new_weight = call(
+        functools.partial(final_kernel, scale, replicas),
+        (shape(momentum.shape, F32), shape(weight.shape, F32), shape(weight.shape, F32)),
+        vmem(8),
         2 * rows * features * features,
-        rows * features * 16,
-    )(basis, kept, own_rest, near, late)
+        rows * features * 28,
+        [pltpu.VMEM((3, rows, features), F32), pltpu.SemaphoreType.DMA((3,))],
+        HBM,
+    )(basis, kept, own_rest, near, late, weight, paired, over_rep(paired, 2))
 
     joined = join(*shares)
     spread = [over_rep(joined, e) for e in range(1, replicas)]
-    gathered = join(joined, *spread)
-    pieces = [half, gathered, swap(half), swap(gathered)]
+    front, gathered = join(half, joined), join(*spread)
+    out = (shape((count, width), BF16),)
+    kernel = functools.partial(early_kernel, replicas, rows)
+    copies = CORES * (1 + len(ARRIVAL))
+    scratch = [
+        pltpu.VMEM((count, CORES * front.shape[0]), BF16),
+        pltpu.SemaphoreType.DMA((copies,)),
+    ]
+    (part_grad,) = call(
+        kernel, out, vmem(3), count * width * features, count * width, scratch, HBM
+    )(cotangent, front, swap(front))
+    kernel = functools.partial(later_kernel, replicas, rows)
+    copies = CORES * (replicas - 1) * len(ARRIVAL)
+    scratch = [
+        pltpu.VMEM((count, CORES * gathered.shape[0]), BF16),
+        pltpu.SemaphoreType.DMA((copies,)),
+    ]
+    specs = [HBM] + vmem(3)
     (input_grad,) = call(
-        functools.partial(input_kernel, chips, replicas),
-        (shape((count, width), BF16),),
-        vmem(1 + len(pieces)),
-        2 * count * width * features,
-        2 * (count + features) * width,
-    )(cotangent, *pieces)
+        kernel, out, specs, count * width * features, count * width, scratch, HBM, {0: 0}
+    )(part_grad, cotangent, gathered, swap(gathered))
     return input_grad, new_momentum, update, new_weight
 
 

time: 55.8 us -> 54.7 us (0.980)
  waiting for transfers between devices: 27.6 us -> 26.6 us
    ppermute x17, waiting for transfers between devices: 27.6 us -> 26.6 us  [permute(): return lax.ppermute(x, axis, pairs)]
  transfers between devices with their start and end apart: 17 -> 17, of which waited for: 10 -> 10; matrix products, arithmetic and copies ran while one was open for 0% -> 0% of each run, Pallas kernels for 12% -> 10%
where the time goes in v3:
time: 54.7 us; the launch traced here: 54.5 us
  waiting for transfers between devices  26.6 us (49%)
  starting transfers between devices  20 us (37%)
  Pallas kernels  7.15 us (13%)
  between operations  0.75 us (1%)
    ppermute x17, waiting for transfers between devices, permute(): return lax.ppermute(x, axis, pairs)  26.6 us
    ppermute x17, starting transfers between devices, permute(): return lax.ppermute(x, axis, pairs)  20 us
    pallas_call x1, Pallas kernels, tuned(): call(functools.partial(final_kernel, scale, replicas), (shape(momentum.sh...  1.55 us
    pallas_call x1, Pallas kernels, tuned(): call(start_kernel, (shape((rows, features), BF16), shape((part, features)...  1.53 us
    pallas_call x1, Pallas kernels, tuned(): call(kernel, out, specs, count * width * features, count * width, scratch...  1.36 us
    pallas_call x1, Pallas kernels, tuned(): call(kernel, out, vmem(3), count * width * features, count * width, scrat...  1.17 us
  transfers between devices with their start and end apart: 17, of which 10 were waited for; matrix products, arithmetic and copies ran while one was open for 0% of the time, Pallas kernels for 10%

profile of v3, /device:TPU:0, one launch (start us, length us, event | category | flops | bytes accessed | tf_op | source)
XLA Modules:
  0.0 54.5 jit_solution(16116607125574545265)
XLA Ops:
  0.6 0.6 %collective-permute-start.9 = (bf16[192,4096]{1,0:T(8,128)(2,1)}, bf16[192,4096]{1,0:T(8,128)(2,1)S(1)}, u32[]{:S(2)}, u32[]{:S(2)}) collective-permute-start(bf16[192,4096]{1,0:T(8,128)(2,1)} %tokens.1), channel_id=1, source_target_pairs={{0,1},{1,0},{2,3},{3,2},{4,5},{5,4},{6,7},{7,6},{8,9},{9,8},{10,11... | collective-permute-start | bytes 4718600 | tf_op jit(solution)/shard_map/ppermute | solution.py:253
  1.2 1.5 %shard_map.93 = (bf16[512,256]{1,0:T(8,128)(2,1)S(1)}, bf16[128,256]{1,0:T(8,128)(2,1)S(1)}, f32[256,256]{1,0:T(8,128)S(1)}, bf16[256,192]{1,0:T(8,128)(2,1)S(1)}, bf16[192,2048]{1,0:T(8,128)(2,1)S(1)}) custom-call(s32[64]{0:T(128)} %order.1, f32[64,256]{1,0:T(8,128)} %constant.2.clone.rows, f32[512,256]{1,0:T(8,128)} %weight.3, bf16[192,256]{1,0:T(8,128)(2,1)} %cot.5, ...), custom_call_target="tpu_custom_call" | custom-call | flops 150994944 | bytes 1572864 | tf_op jit(solution)/shard_map/pallas_call | solution.py:273
  2.7 2.6 %collective-permute-start = (bf16[128,256]{1,0:T(8,128)(2,1)S(1)}, bf16[128,256]{1,0:T(8,128)(2,1)S(1)}, u32[]{:S(2)}, u32[]{:S(2)}) collective-permute-start(bf16[128,256]{1,0:T(8,128)(2,1)S(1)} %get-tuple-element.22), channel_id=1, source_target_pairs={{0,2},{1,3},{2,0},{3,1},{4,6},{5,7},{6,4},{7,5},{8,10},{9,11},{10,... | collective-permute-start | bytes 196616 | tf_op jit(solution)/shard_map/ppermute | solution.py:253
  5.4 2.6 %collective-permute-start.1 = (bf16[128,256]{1,0:T(8,128)(2,1)S(1)}, bf16[128,256]{1,0:T(8,128)(2,1)S(1)}, u32[]{:S(2)}, u32[]{:S(2)}) collective-permute-start(bf16[128,256]{1,0:T(8,128)(2,1)S(1)} %get-tuple-element.22), channel_id=1, source_target_pairs={{0,4},{1,5},{2,6},{3,7},{4,0},{5,1},{6,2},{7,3},{8,12},{9,13},{10,... | collective-permute-start | bytes 196616 | tf_op jit(solution)/shard_map/ppermute | solution.py:253
  8.0 0.0 collective-permute-start.2
  8.0 0.2 collective-permute-done.refs_0_
  8.1 4.3 %collective-permute-done.1.refs_1_ = bf16[128,256]{1,0:T(8,128)(2,1)S(1)} collective-permute-done((bf16[128,256]{1,0:T(8,128)(2,1)S(1)}, bf16[128,256]{1,0:T(8,128)(2,1)S(1)}, u32[]{:S(2)}, u32[]{:S(2)}) %collective-permute-start.1) | collective-permute-done | bytes 65568 | tf_op jit(solution)/shard_map/ppermute | solution.py:253
  12.4 1.6 %collective-permute-done.2.refs_2_ = bf16[128,256]{1,0:T(8,128)(2,1)S(1)} collective-permute-done((bf16[128,256]{1,0:T(8,128)(2,1)S(1)}, bf16[128,256]{1,0:T(8,128)(2,1)S(1)}, u32[]{:S(2)}, u32[]{:S(2)}) %collective-permute-start.2) | collective-permute-done | bytes 65568 | tf_op jit(solution)/shard_map/ppermute | solution.py:253
  14.0 1.6 %collective-permute-start.4 = (bf16[384,256]{1,0:T(8,128)(2,1)S(1)}, bf16[384,256]{1,0:T(8,128)(2,1)S(1)}, u32[]{:S(2)}, u32[]{:S(2)}) collective-permute-start(bf16[384,256]{1,0:T(8,128)(2,1)S(1)} %shard_map.94.refs_1_), channel_id=1, source_target_pairs={{0,8},{8,0},{16,24},{24,16},{1,9},{9,1},{17,25},{25,17},{2,10},{10... | collective-permute-start | bytes 589832 | tf_op jit(solution)/shard_map/ppermute | solution.py:253
  15.6 1.5 %collective-permute-start.5 = (bf16[384,256]{1,0:T(8,128)(2,1)S(1)}, bf16[384,256]{1,0:T(8,128)(2,1)S(1)}, u32[]{:S(2)}, u32[]{:S(2)}) collective-permute-start(bf16[384,256]{1,0:T(8,128)(2,1)S(1)} %shard_map.94.refs_1_), channel_id=1, source_target_pairs={{0,16},{8,24},{16,0},{24,8},{1,17},{9,25},{17,1},{25,9},{2,18},{10... | collective-permute-start | bytes 589832 | tf_op jit(solution)/shard_map/ppermute | solution.py:253
  17.1 0.5 collective-permute-start.6
  17.6 4.0 %collective-permute-done.4.refs_0_ = bf16[384,256]{1,0:T(8,128)(2,1)S(1)} collective-permute-done((bf16[384,256]{1,0:T(8,128)(2,1)S(1)}, bf16[384,256]{1,0:T(8,128)(2,1)S(1)}, u32[]{:S(2)}, u32[]{:S(2)}) %collective-permute-start.4) | collective-permute-done | bytes 196640 | tf_op jit(solution)/shard_map/ppermute | solution.py:253
  21.6 3.8 %collective-permute-done.5.refs_1_ = bf16[384,256]{1,0:T(8,128)(2,1)S(1)} collective-permute-done((bf16[384,256]{1,0:T(8,128)(2,1)S(1)}, bf16[384,256]{1,0:T(8,128)(2,1)S(1)}, u32[]{:S(2)}, u32[]{:S(2)}) %collective-permute-start.5) | collective-permute-done | bytes 196640 | tf_op jit(solution)/shard_map/ppermute | solution.py:253
  25.4 0.0 collective-permute-done.6.refs_2_
  25.4 0.1 collective-permute-start.7
  25.5 0.5 collective-permute-start.8
  26.0 0.1 collective-permute-start.3
  26.2 1.5 %collective-permute-done.8.theirs = bf16[256,192]{1,0:T(8,128)(2,1)S(1)} collective-permute-done((bf16[256,192]{1,0:T(8,128)(2,1)S(1)}, bf16[256,192]{1,0:T(8,128)(2,1)S(1)}, u32[]{:S(2)}, u32[]{:S(2)}) %collective-permute-start.8) | collective-permute-done | bytes 98336 | tf_op jit(solution)/shard_map/ppermute | solution.py:253
  27.7 0.0 collective-permute-done.9.their_tok
  27.7 0.0 copy-start.2
  27.7 0.7 %shard_map.100 = (bf16[128,512]{1,0:T(8,128)(2,1)S(1)}, f32[64,512]{1,0:T(8,128)S(1)}, f32[64,512]{1,0:T(8,128)S(1)}, bf16[192,512]{1,0:T(8,128)(2,1)S(1)}, bf16...) custom-call(bf16[256,192]{1,0:T(8,128)(2,1)S(1)} %get-tuple-element.25.mine, ...), custom_call_target="tpu_custom_call" | custom-call | flops 402653184 | bytes 1572864 | tf_op jit(solution)/shard_map/pallas_call | solution.py:299
  28.4 0.0 copy-start.1
  28.4 2.0 %collective-permute-start.11 = (bf16[192,512]{1,0:T(8,128)(2,1)S(1)}, bf16[192,512]{1,0:T(8,128)(2,1)S(1)}, u32[]{:S(2)}, u32[]{:S(2)}) collective-permute-start(bf16[192,512]{1,0:T(8,128)(2,1)S(1)} %get-tuple-element.30), channel_id=1, source_target_pairs={{0,2},{1,3},{2,0},{3,1},{4,6},{5,7},{6,4},{7,5},{8,10},{9,11},{10,... | collective-permute-start | bytes 589832 | tf_op jit(solution)/shard_map/ppermute | solution.py:253
  30.4 0.1 collective-permute-start.13
  30.5 7.9 %collective-permute-done.13.arrived = bf16[128,512]{1,0:T(8,128)(2,1)S(1)} collective-permute-done((bf16[128,512]{1,0:T(8,128)(2,1)S(1)}, bf16[128,512]{1,0:T(8,128)(2,1)S(1)}, u32[]{:S(2)}, u32[]{:S(2)}) %collective-permute-start.13) | collective-permute-done | bytes 131104 | tf_op jit(solution)/shard_map/ppermute | solution.py:253
  38.4 2.2 %collective-permute-start.14 = (bf16[64,512]{1,0:T(8,128)(2,1)S(1)}, bf16[64,512]{1,0:T(8,128)(2,1)S(1)}, u32[]{:S(2)}, u32[]{:S(2)}) collective-permute-start(bf16[64,512]{1,0:T(8,128)(2,1)S(1)} %shard_map.102), channel_id=1, source_target_pairs={{0,4},{1,5},{2,6},{3,7},{4,0},{5,1},{6,2},{7,3},{8,12},{9,13},{10,... | collective-permute-start | bytes 196616 | tf_op jit(solution)/shard_map/ppermute | solution.py:253
  40.6 0.3 collective-permute-start.10
  40.9 0.0 collective-permute-done.11.arrived
  41.0 2.3 %collective-permute-start.12 = (bf16[192,512]{1,0:T(8,128)(2,1)S(1)}, bf16[192,512]{1,0:T(8,128)(2,1)S(1)}, u32[]{:S(2)}, u32[]{:S(2)}) collective-permute-start(bf16[192,512]{1,0:T(8,128)(2,1)S(1)} %shard_map.101), channel_id=1, source_target_pairs={{0,4},{1,5},{2,6},{3,7},{4,0},{5,1},{6,2},{7,3},{8,12},{9,13},{10,... | collective-permute-start | bytes 589832 | tf_op jit(solution)/shard_map/ppermute | solution.py:253
  43.3 0.0 copy-done.2
  43.3 0.7 %shard_map.99 = (f32[512,256]{1,0:T(8,128)S(1)}, f32[64,512]{1,0:T(8,128)S(1)}) custom-call(f32[256,256]{1,0:T(8,128)S(1)} %get-tuple-element.23.basis, f32[1,512,256]{2,1,0:T(8,128)S(1)} %copy-done.2), custom_call_target="tpu_custom_call" | custom-call | flops 201326592 | bytes 1048576 | tf_op jit(solution)/shard_map/pallas_call | solution.py:313
  43.9 0.3 collective-permute-done.14.late
  44.3 1.4 %collective-permute-start.15 = (bf16[64,512]{1,0:T(8,128)(2,1)S(1)}, bf16[64,512]{1,0:T(8,128)(2,1)S(1)}, u32[]{:S(2)}, u32[]{:S(2)}) collective-permute-start(bf16[64,512]{1,0:T(8,128)(2,1)S(1)} %shard_map.103.left), channel_id=1, source_target_pairs={{0,8},{8,0},{16,24},{24,16},{1,9},{9,1},{17,25},{25,17},{2,10},{10... | collective-permute-start | bytes 196616 | tf_op jit(solution)/shard_map/ppermute | solution.py:253
  45.7 2.9 %collective-permute-done.15.right = bf16[64,512]{1,0:T(8,128)(2,1)S(1)} collective-permute-done((bf16[64,512]{1,0:T(8,128)(2,1)S(1)}, bf16[64,512]{1,0:T(8,128)(2,1)S(1)}, u32[]{:S(2)}, u32[]{:S(2)}) %collective-permute-start.15) | collective-permute-done | bytes 65568 | tf_op jit(solution)/shard_map/ppermute | solution.py:253
  48.7 1.6 %collective-permute-start.16 = (bf16[64,512]{1,0:T(8,128)(2,1)S(1)}, bf16[64,512]{1,0:T(8,128)(2,1)S(1)}, u32[]{:S(2)}, u32[]{:S(2)}) collective-permute-start(bf16[64,512]{1,0:T(8,128)(2,1)S(1)} %shard_map.104.left), channel_id=1, source_target_pairs={{0,16},{8,24},{16,0},{24,8},{1,17},{9,25},{17,1},{25,9},{2,18},{10... | collective-permute-start | bytes 196616 | tf_op jit(solution)/shard_map/ppermute | solution.py:253
  50.3 0.0 collective-permute-done.3.theirs
  50.3 0.0 copy-done.1
  50.3 1.2 %shard_map.96._ = bf16[192,4096]{1,0:T(8,128)(2,1)} custom-call(bf16[192,256]{1,0:T(8,128)(2,1)S(1)} %copy-done.1, bf16[896,256]{1,0:T(8,128)(2,1)S(1)} %shard_map.95.mine, bf16[896,256]{1,0:T(8,128)(2,1)S(1)} %collective-permute-done.3.theirs), custom_call_target="tpu_custom_call" | custom-call | flops 201326592 | bytes 786432 | tf_op jit(solution)/shard_map/pallas_call | solution.py:343
  51.5 0.0 copy-start
  51.5 0.0 collective-permute-done.7.theirs
  51.5 1.4 %shard_map.98 = bf16[192,4096]{1,0:T(8,128)(2,1)} custom-call(bf16[192,4096]{1,0:T(8,128)(2,1)} %shard_map.96._, bf16[192,256]{1,0:T(8,128)(2,1)S(1)} %copy-done.1, bf16[1152,256]{1,0:T(8,128)(2,1)S(1)} %shard_map.97.mine, bf16[1152,256]{1,0:T(8,128)(2,1)S(1)} %collective-permute-done.7.theirs), custom_call_target="tpu_custom_call", output_to_operand_aliasing={{}: (0, {})} | custom-call | flops 201326592 | bytes 786432 | tf_op jit(solution)/shard_map/pallas_call | solution.py:353
  52.9 0.0 collective-permute-done.10.near
  52.9 0.1 collective-permute-done.16.right
  53.0 0.0 collective-permute-done.12.late
  53.0 0.0 copy-done
  53.0 1.5 %shard_map.105 = (f32[1,512,256]{2,1,0:T(8,128)}, f32[512,256]{1,0:T(8,128)}, f32[512,256]{1,0:T(8,128)}) custom-call(f32[256,256]{1,0:T(8,128)S(1)} %get-tuple-element.23.basis, f32[512,256]{1,0:T(8,128)S(1)} %get-tuple-element.24.kept, f32[192,512]{1,0:T(8,128)S(1)} %get-tuple-element.27.own, bf16[192,512]{1,0:T(8,128)(2,1)S(1)} %collective-permute-done.10.near, ...), custom_call_target="tpu_custom_call" | custom-call | flops 67108864 | bytes 3670016 | tf_op jit(solution)/shard_map/pallas_call | solution.py:323
  (7 shorter events, 0.2 us)
Async XLA Ops:
  0.6 27.0 %collective-permute-start.9 = (bf16[192,4096]{1,0:T(8,128)(2,1)}, bf16[192,4096]{1,0:T(8,128)(2,1)S(1)}, u32[]{:S(2)}, u32[]{:S(2)}) collective-permute-start(bf16[192,4096]{1,0:T(8,128)(2,1)} %tokens.1), channel_id=1, source_target_pairs={{0,1},{1,0},{2,3},{3,2},{4,5},{5,4},{6,7},{7,6},{8,9},{9,8},{10,11... | collective-permute-start | bytes 4718600 | tf_op jit(solution)/shard_map/ppermute | solution.py:253
  2.7 5.4 %collective-permute-start = (bf16[128,256]{1,0:T(8,128)(2,1)S(1)}, bf16[128,256]{1,0:T(8,128)(2,1)S(1)}, u32[]{:S(2)}, u32[]{:S(2)}) collective-permute-start(bf16[128,256]{1,0:T(8,128)(2,1)S(1)} %get-tuple-element.22), channel_id=1, source_target_pairs={{0,2},{1,3},{2,0},{3,1},{4,6},{5,7},{6,4},{7,5},{8,10},{9,11},{10,... | collective-permute-start | bytes 196616 | tf_op jit(solution)/shard_map/ppermute | solution.py:253
  5.4 7.0 %collective-permute-start.1 = (bf16[128,256]{1,0:T(8,128)(2,1)S(1)}, bf16[128,256]{1,0:T(8,128)(2,1)S(1)}, u32[]{:S(2)}, u32[]{:S(2)}) collective-permute-start(bf16[128,256]{1,0:T(8,128)(2,1)S(1)} %get-tuple-element.22), channel_id=1, source_target_pairs={{0,4},{1,5},{2,6},{3,7},{4,0},{5,1},{6,2},{7,3},{8,12},{9,13},{10,... | collective-permute-start | bytes 196616 | tf_op jit(solution)/shard_map/ppermute | solution.py:253
  8.0 6.1 %collective-permute-start.2 = (bf16[128,256]{1,0:T(8,128)(2,1)S(1)}, bf16[128,256]{1,0:T(8,128)(2,1)S(1)}, u32[]{:S(2)}, u32[]{:S(2)}) collective-permute-start(bf16[128,256]{1,0:T(8,128)(2,1)S(1)} %get-tuple-element.22), channel_id=1, source_target_pairs={{0,6},{1,7},{2,4},{3,5},{4,2},{5,3},{6,0},{7,1},{8,14},{9,15},{10,... | collective-permute-start | bytes 196616 | tf_op jit(solution)/shard_map/ppermute | solution.py:253
  14.0 7.6 %collective-permute-start.4 = (bf16[384,256]{1,0:T(8,128)(2,1)S(1)}, bf16[384,256]{1,0:T(8,128)(2,1)S(1)}, u32[]{:S(2)}, u32[]{:S(2)}) collective-permute-start(bf16[384,256]{1,0:T(8,128)(2,1)S(1)} %shard_map.94.refs_1_), channel_id=1, source_target_pairs={{0,8},{8,0},{16,24},{24,16},{1,9},{9,1},{17,25},{25,17},{2,10},{10... | collective-permute-start | bytes 589832 | tf_op jit(solution)/shard_map/ppermute | solution.py:253
  15.6 9.8 %collective-permute-start.5 = (bf16[384,256]{1,0:T(8,128)(2,1)S(1)}, bf16[384,256]{1,0:T(8,128)(2,1)S(1)}, u32[]{:S(2)}, u32[]{:S(2)}) collective-permute-start(bf16[384,256]{1,0:T(8,128)(2,1)S(1)} %shard_map.94.refs_1_), channel_id=1, source_target_pairs={{0,16},{8,24},{16,0},{24,8},{1,17},{9,25},{17,1},{25,9},{2,18},{10... | collective-permute-start | bytes 589832 | tf_op jit(solution)/shard_map/ppermute | solution.py:253
  17.1 8.3 %collective-permute-start.6 = (bf16[384,256]{1,0:T(8,128)(2,1)S(1)}, bf16[384,256]{1,0:T(8,128)(2,1)S(1)}, u32[]{:S(2)}, u32[]{:S(2)}) collective-permute-start(bf16[384,256]{1,0:T(8,128)(2,1)S(1)} %shard_map.94.refs_1_), channel_id=1, source_target_pairs={{0,24},{8,16},{16,8},{24,0},{1,25},{9,17},{17,9},{25,1},{2,26},{10... | collective-permute-start | bytes 589832 | tf_op jit(solution)/shard_map/ppermute | solution.py:253
  25.4 26.1 %collective-permute-start.7 = (bf16[1152,256]{1,0:T(8,128)(2,1)S(1)}, bf16[1152,256]{1,0:T(8,128)(2,1)S(1)}, u32[]{:S(2)}, u32[]{:S(2)}) collective-permute-start(bf16[1152,256]{1,0:T(8,128)(2,1)S(1)} %shard_map.97.mine), channel_id=1, source_target_pairs={{0,1},{1,0},{2,3},{3,2},{4,5},{5,4},{6,7},{7,6},{8,9},{9,8},{10,11... | collective-permute-start | bytes 1769480 | tf_op jit(solution)/shard_map/ppermute | solution.py:253
  25.5 2.2 %collective-permute-start.8 = (bf16[256,192]{1,0:T(8,128)(2,1)S(1)}, bf16[256,192]{1,0:T(8,128)(2,1)S(1)}, u32[]{:S(2)}, u32[]{:S(2)}) collective-permute-start(bf16[256,192]{1,0:T(8,128)(2,1)S(1)} %get-tuple-element.25.mine), channel_id=1, source_target_pairs={{0,1},{1,0},{2,3},{3,2},{4,5},{5,4},{6,7},{7,6},{8,9},{9,8},{10,11... | collective-permute-start | bytes 294920 | tf_op jit(solution)/shard_map/ppermute | solution.py:253
  26.0 24.3 %collective-permute-start.3 = (bf16[896,256]{1,0:T(8,128)(2,1)S(1)}, bf16[896,256]{1,0:T(8,128)(2,1)S(1)}, u32[]{:S(2)}, u32[]{:S(2)}) collective-permute-start(bf16[896,256]{1,0:T(8,128)(2,1)S(1)} %shard_map.95.mine), channel_id=1, source_target_pairs={{0,1},{1,0},{2,3},{3,2},{4,5},{5,4},{6,7},{7,6},{8,9},{9,8},{10,11... | collective-permute-start | bytes 1376264 | tf_op jit(solution)/shard_map/ppermute | solution.py:253
  27.7 15.6 %copy-start.2 = (f32[1,512,256]{2,1,0:T(8,128)S(1)}, f32[1,512,256]{2,1,0:T(8,128)}, u32[]{:S(2)}) copy-start(f32[1,512,256]{2,1,0:T(8,128)} %momentum.1) | copy-start | bytes 1572868
  28.4 21.9 %copy-start.1 = (bf16[192,256]{1,0:T(8,128)(2,1)S(1)}, bf16[192,256]{1,0:T(8,128)(2,1)}, u32[]{:S(2)}) copy-start(bf16[192,256]{1,0:T(8,128)(2,1)} %cot.5) | copy-start | bytes 294916
  28.4 12.5 %collective-permute-start.11 = (bf16[192,512]{1,0:T(8,128)(2,1)S(1)}, bf16[192,512]{1,0:T(8,128)(2,1)S(1)}, u32[]{:S(2)}, u32[]{:S(2)}) collective-permute-start(bf16[192,512]{1,0:T(8,128)(2,1)S(1)} %get-tuple-element.30), channel_id=1, source_target_pairs={{0,2},{1,3},{2,0},{3,1},{4,6},{5,7},{6,4},{7,5},{8,10},{9,11},{10,... | collective-permute-start | bytes 589832 | tf_op jit(solution)/shard_map/ppermute | solution.py:253
  30.4 8.0 %collective-permute-start.13 = (bf16[128,512]{1,0:T(8,128)(2,1)S(1)}, bf16[128,512]{1,0:T(8,128)(2,1)S(1)}, u32[]{:S(2)}, u32[]{:S(2)}) collective-permute-start(bf16[128,512]{1,0:T(8,128)(2,1)S(1)} %get-tuple-element.33), channel_id=1, source_target_pairs={{0,2},{1,3},{2,0},{3,1},{4,6},{5,7},{6,4},{7,5},{8,10},{9,11},{10,... | collective-permute-start | bytes 393224 | tf_op jit(solution)/shard_map/ppermute | solution.py:253
  38.4 5.8 %collective-permute-start.14 = (bf16[64,512]{1,0:T(8,128)(2,1)S(1)}, bf16[64,512]{1,0:T(8,128)(2,1)S(1)}, u32[]{:S(2)}, u32[]{:S(2)}) collective-permute-start(bf16[64,512]{1,0:T(8,128)(2,1)S(1)} %shard_map.102), channel_id=1, source_target_pairs={{0,4},{1,5},{2,6},{3,7},{4,0},{5,1},{6,2},{7,3},{8,12},{9,13},{10,... | collective-permute-start | bytes 196616 | tf_op jit(solution)/shard_map/ppermute | solution.py:253
  40.6 12.3 %collective-permute-start.10 = (bf16[192,512]{1,0:T(8,128)(2,1)S(1)}, bf16[192,512]{1,0:T(8,128)(2,1)S(1)}, u32[]{:S(2)}, u32[]{:S(2)}) collective-permute-start(bf16[192,512]{1,0:T(8,128)(2,1)S(1)} %get-tuple-element.28), channel_id=1, source_target_pairs={{0,2},{1,3},{2,0},{3,1},{4,6},{5,7},{6,4},{7,5},{8,10},{9,11},{10,... | collective-permute-start | bytes 589832 | tf_op jit(solution)/shard_map/ppermute | solution.py:253
  41.0 12.0 %collective-permute-start.12 = (bf16[192,512]{1,0:T(8,128)(2,1)S(1)}, bf16[192,512]{1,0:T(8,128)(2,1)S(1)}, u32[]{:S(2)}, u32[]{:S(2)}) collective-permute-start(bf16[192,512]{1,0:T(8,128)(2,1)S(1)} %shard_map.101), channel_id=1, source_target_pairs={{0,4},{1,5},{2,6},{3,7},{4,0},{5,1},{6,2},{7,3},{8,12},{9,13},{10,... | collective-permute-start | bytes 589832 | tf_op jit(solution)/shard_map/ppermute | solution.py:253
  44.3 4.3 %collective-permute-start.15 = (bf16[64,512]{1,0:T(8,128)(2,1)S(1)}, bf16[64,512]{1,0:T(8,128)(2,1)S(1)}, u32[]{:S(2)}, u32[]{:S(2)}) collective-permute-start(bf16[64,512]{1,0:T(8,128)(2,1)S(1)} %shard_map.103.left), channel_id=1, source_target_pairs={{0,8},{8,0},{16,24},{24,16},{1,9},{9,1},{17,25},{25,17},{2,10},{10... | collective-permute-start | bytes 196616 | tf_op jit(solution)/shard_map/ppermute | solution.py:253
  48.7 4.3 %collective-permute-start.16 = (bf16[64,512]{1,0:T(8,128)(2,1)S(1)}, bf16[64,512]{1,0:T(8,128)(2,1)S(1)}, u32[]{:S(2)}, u32[]{:S(2)}) collective-permute-start(bf16[64,512]{1,0:T(8,128)(2,1)S(1)} %shard_map.104.left), channel_id=1, source_target_pairs={{0,16},{8,24},{16,0},{24,8},{1,17},{9,25},{17,1},{25,9},{2,18},{10... | collective-permute-start | bytes 196616 | tf_op jit(solution)/shard_map/ppermute | solution.py:253
  51.5 1.5 %copy-start = (f32[512,256]{1,0:T(8,128)S(1)}, f32[512,256]{1,0:T(8,128)}, u32[]{:S(2)}) copy-start(f32[512,256]{1,0:T(8,128)} %weight.3) | copy-start | bytes 1572868

commit v4 on v3

--- a/solution.py
+++ b/solution.py
@@ -172,12 +172,8 @@
     out[...] = (coded[...] + scale * total).astype(out.dtype)
 
 
-def add_kernel(left, right, out):
-    out[...] = (wide(left) + wide(right)).astype(out.dtype)
-
-
-def final_kernel(scale, replicas, basis, kept, own, near, late, weight, left, right, *refs):
-    (moment, update, new_weight), (stage, sems) = refs[:3], refs[3:]
+def final_kernel(scale, replicas, basis, kept, own, near, late, weight, *refs):
+    codes, (moment, update, new_weight, stage, sems) = refs[:-5], refs[-5:]
     total = own[...] + wide(near) + wide(late)
     rest = basis[basis.shape[0] - own.shape[0] :, :]
     grad = dot(total.astype(BF16), rest.astype(BF16), ((0,), (0,)))
@@ -188,7 +184,8 @@
         pltpu.make_async_copy(stage.at[2], new_weight, sems.at[2]),
     ]
     copies[0].start()
-    code = wide(left) + wide(right)
+    pairs = [wide(a) + wide(b) for a, b in zip(codes[::2], codes[1::2])]
+    code = sum(pairs[1:], pairs[0])
     value = outer(code, basis[: code.shape[0], :]) * (1.0 / replicas)
     stage[1] = value
     copies[1].start()
@@ -319,16 +316,16 @@
     )(basis, momentum)
     scale = float(count * members) ** (-0.5)
     packed = simple(functools.partial(pack_kernel, scale), code, coded, own_code, codes, late_code)
-    paired = simple(add_kernel, code, packed, over_rep(packed, 1))
+    codes = [packed] + [over_rep(packed, e) for e in range(1, replicas)]
     new_momentum, update, new_weight = call(
         functools.partial(final_kernel, scale, replicas),
         (shape(momentum.shape, F32), shape(weight.shape, F32), shape(weight.shape, F32)),
-        vmem(8),
+        vmem(6 + replicas),
         2 * rows * features * features,
         rows * features * 28,
         [pltpu.VMEM((3, rows, features), F32), pltpu.SemaphoreType.DMA((3,))],
         HBM,
-    )(basis, kept, own_rest, near, late, weight, paired, over_rep(paired, 2))
+    )(basis, kept, own_rest, near, late, weight, *codes)
 
     joined = join(*shares)
     spread = [over_rep(joined, e) for e in range(1, replicas)]

time: 54.7 us -> 59.5 us (1.088)
  waiting for transfers between devices: 26.6 us -> 31.3 us
    ppermute x17 -> x18, waiting for transfers between devices: 26.6 us -> 31.3 us  [permute(): return lax.ppermute(x, axis, pairs)]
    ppermute x17 -> x18, starting transfers between devices: 20 us -> 20.1 us  [permute(): return lax.ppermute(x, axis, pairs)]
  transfers between devices with their start and end apart: 17 -> 18, of which waited for: 10 -> 10; matrix products, arithmetic and copies ran while one was open for 0% -> 0% of each run, Pallas kernels for 10% -> 9%
where the time goes in v4:
time: 59.5 us; the launch traced here: 59.3 us
  waiting for transfers between devices  31.3 us (53%)
  starting transfers between devices  20.1 us (34%)
  Pallas kernels  7.14 us (12%)
  between operations  0.77 us (1%)
    ppermute x18, waiting for transfers between devices, permute(): return lax.ppermute(x, axis, pairs)  31.3 us
    ppermute x18, starting transfers between devices, permute(): return lax.ppermute(x, axis, pairs)  20.1 us
    pallas_call x1, Pallas kernels, tuned(): call(functools.partial(final_kernel, scale, replicas), (shape(momentum.sh...  1.55 us
    pallas_call x1, Pallas kernels, tuned(): call(start_kernel, (shape((rows, features), BF16), shape((part, features)...  1.53 us
    pallas_call x1, Pallas kernels, tuned(): call(kernel, out, specs, count * width * features, count * width, scratch...  1.36 us
  transfers between devices with their start and end apart: 18, of which 10 were waited for; matrix products, arithmetic and copies ran while one was open for 0% of the time, Pallas kernels for 9%

profile of v4, /device:TPU:0, one launch (start us, length us, event | category | flops | bytes accessed | tf_op | source)
XLA Modules:
  0.0 59.3 jit_solution(2668995216206204774)
XLA Ops:
  0.6 0.6 collective-permute-start.9
  1.2 1.5 %shard_map.93 = (bf16[512,256]{1,0:T(8,128)(2,1)S(1)}, bf16[128,256]{1,0:T(8,128)(2,1)S(1)}, f32[256,256]{1,0:T(8,128)S(1)}, bf16[256,192]{1,0:T(8,128)(2,1)S(1)}, bf16[192,2048]{1,0:T(8,128)(2,1)S(1)}) custom-call(s32[64]{0:T(128)} %order.1, f32[64,256]{1,0:T(8,128)} %constant.2.clone.rows, f32[512,256]{1,0:T(8,128)} %weight.3, bf16[192,256]{1,0:T(8,128)(2,1)} %cot.5, ...), custom_call_target="tpu_custom_call" | custom-call | flops 150994944 | bytes 1572864 | tf_op jit(solution)/shard_map/pallas_call | solution.py:270
  2.7 2.6 %collective-permute-start = (bf16[128,256]{1,0:T(8,128)(2,1)S(1)}, bf16[128,256]{1,0:T(8,128)(2,1)S(1)}, u32[]{:S(2)}, u32[]{:S(2)}) collective-permute-start(bf16[128,256]{1,0:T(8,128)(2,1)S(1)} %get-tuple-element.22), channel_id=1, source_target_pairs={{0,2},{1,3},{2,0},{3,1},{4,6},{5,7},{6,4},{7,5},{8,10},{9,11},{10,... | collective-permute-start | bytes 196616 | tf_op jit(solution)/shard_map/ppermute | solution.py:250
  5.4 2.6 %collective-permute-start.1 = (bf16[128,256]{1,0:T(8,128)(2,1)S(1)}, bf16[128,256]{1,0:T(8,128)(2,1)S(1)}, u32[]{:S(2)}, u32[]{:S(2)}) collective-permute-start(bf16[128,256]{1,0:T(8,128)(2,1)S(1)} %get-tuple-element.22), channel_id=1, source_target_pairs={{0,4},{1,5},{2,6},{3,7},{4,0},{5,1},{6,2},{7,3},{8,12},{9,13},{10,... | collective-permute-start | bytes 196616 | tf_op jit(solution)/shard_map/ppermute | solution.py:250
  8.0 0.0 collective-permute-start.2
  8.0 0.2 collective-permute-done.refs_0_
  8.1 4.3 %collective-permute-done.1.refs_1_ = bf16[128,256]{1,0:T(8,128)(2,1)S(1)} collective-permute-done((bf16[128,256]{1,0:T(8,128)(2,1)S(1)}, bf16[128,256]{1,0:T(8,128)(2,1)S(1)}, u32[]{:S(2)}, u32[]{:S(2)}) %collective-permute-start.1) | collective-permute-done | bytes 65568 | tf_op jit(solution)/shard_map/ppermute | solution.py:250
  12.4 1.6 %collective-permute-done.2.refs_2_ = bf16[128,256]{1,0:T(8,128)(2,1)S(1)} collective-permute-done((bf16[128,256]{1,0:T(8,128)(2,1)S(1)}, bf16[128,256]{1,0:T(8,128)(2,1)S(1)}, u32[]{:S(2)}, u32[]{:S(2)}) %collective-permute-start.2) | collective-permute-done | bytes 65568 | tf_op jit(solution)/shard_map/ppermute | solution.py:250
  14.0 1.6 %collective-permute-start.4 = (bf16[384,256]{1,0:T(8,128)(2,1)S(1)}, bf16[384,256]{1,0:T(8,128)(2,1)S(1)}, u32[]{:S(2)}, u32[]{:S(2)}) collective-permute-start(bf16[384,256]{1,0:T(8,128)(2,1)S(1)} %shard_map.94.refs_1_), channel_id=1, source_target_pairs={{0,8},{8,0},{16,24},{24,16},{1,9},{9,1},{17,25},{25,17},{2,10},{10... | collective-permute-start | bytes 589832 | tf_op jit(solution)/shard_map/ppermute | solution.py:250
  15.6 1.5 %collective-permute-start.5 = (bf16[384,256]{1,0:T(8,128)(2,1)S(1)}, bf16[384,256]{1,0:T(8,128)(2,1)S(1)}, u32[]{:S(2)}, u32[]{:S(2)}) collective-permute-start(bf16[384,256]{1,0:T(8,128)(2,1)S(1)} %shard_map.94.refs_1_), channel_id=1, source_target_pairs={{0,16},{8,24},{16,0},{24,8},{1,17},{9,25},{17,1},{25,9},{2,18},{10... | collective-permute-start | bytes 589832 | tf_op jit(solution)/shard_map/ppermute | solution.py:250
  17.1 0.5 collective-permute-start.6
  17.6 4.0 %collective-permute-done.4.refs_0_ = bf16[384,256]{1,0:T(8,128)(2,1)S(1)} collective-permute-done((bf16[384,256]{1,0:T(8,128)(2,1)S(1)}, bf16[384,256]{1,0:T(8,128)(2,1)S(1)}, u32[]{:S(2)}, u32[]{:S(2)}) %collective-permute-start.4) | collective-permute-done | bytes 196640 | tf_op jit(solution)/shard_map/ppermute | solution.py:250
  21.6 3.8 %collective-permute-done.5.refs_1_ = bf16[384,256]{1,0:T(8,128)(2,1)S(1)} collective-permute-done((bf16[384,256]{1,0:T(8,128)(2,1)S(1)}, bf16[384,256]{1,0:T(8,128)(2,1)S(1)}, u32[]{:S(2)}, u32[]{:S(2)}) %collective-permute-start.5) | collective-permute-done | bytes 196640 | tf_op jit(solution)/shard_map/ppermute | solution.py:250
  25.4 0.0 collective-permute-done.6.refs_2_
  25.4 0.1 collective-permute-start.7
  25.5 0.5 collective-permute-start.8
  26.0 0.1 collective-permute-start.3
  26.2 1.5 %collective-permute-done.8.theirs = bf16[256,192]{1,0:T(8,128)(2,1)S(1)} collective-permute-done((bf16[256,192]{1,0:T(8,128)(2,1)S(1)}, bf16[256,192]{1,0:T(8,128)(2,1)S(1)}, u32[]{:S(2)}, u32[]{:S(2)}) %collective-permute-start.8) | collective-permute-done | bytes 98336 | tf_op jit(solution)/shard_map/ppermute | solution.py:250
  27.7 0.0 collective-permute-done.9.their_tok
  27.7 0.0 copy-start.2
  27.7 0.7 %shard_map.100 = (bf16[128,512]{1,0:T(8,128)(2,1)S(1)}, f32[64,512]{1,0:T(8,128)S(1)}, f32[64,512]{1,0:T(8,128)S(1)}, bf16[192,512]{1,0:T(8,128)(2,1)S(1)}, bf16...) custom-call(bf16[256,192]{1,0:T(8,128)(2,1)S(1)} %get-tuple-element.25.mine, ...), custom_call_target="tpu_custom_call" | custom-call | flops 402653184 | bytes 1572864 | tf_op jit(solution)/shard_map/pallas_call | solution.py:296
  28.4 0.0 copy-start.1
  28.4 2.0 %collective-permute-start.11 = (bf16[192,512]{1,0:T(8,128)(2,1)S(1)}, bf16[192,512]{1,0:T(8,128)(2,1)S(1)}, u32[]{:S(2)}, u32[]{:S(2)}) collective-permute-start(bf16[192,512]{1,0:T(8,128)(2,1)S(1)} %get-tuple-element.30), channel_id=1, source_target_pairs={{0,2},{1,3},{2,0},{3,1},{4,6},{5,7},{6,4},{7,5},{8,10},{9,11},{10,... | collective-permute-start | bytes 589832 | tf_op jit(solution)/shard_map/ppermute | solution.py:250
  30.4 0.1 collective-permute-start.13
  30.5 1.9 %collective-permute-start.10 = (bf16[192,512]{1,0:T(8,128)(2,1)S(1)}, bf16[192,512]{1,0:T(8,128)(2,1)S(1)}, u32[]{:S(2)}, u32[]{:S(2)}) collective-permute-start(bf16[192,512]{1,0:T(8,128)(2,1)S(1)} %get-tuple-element.28), channel_id=1, source_target_pairs={{0,2},{1,3},{2,0},{3,1},{4,6},{5,7},{6,4},{7,5},{8,10},{9,11},{10,... | collective-permute-start | bytes 589832 | tf_op jit(solution)/shard_map/ppermute | solution.py:250
  32.4 3.8 %collective-permute-done.11.arrived = bf16[192,512]{1,0:T(8,128)(2,1)S(1)} collective-permute-done((bf16[192,512]{1,0:T(8,128)(2,1)S(1)}, bf16[192,512]{1,0:T(8,128)(2,1)S(1)}, u32[]{:S(2)}, u32[]{:S(2)}) %collective-permute-start.11) | collective-permute-done | bytes 196640 | tf_op jit(solution)/shard_map/ppermute | solution.py:250
  36.3 2.4 %collective-permute-start.12 = (bf16[192,512]{1,0:T(8,128)(2,1)S(1)}, bf16[192,512]{1,0:T(8,128)(2,1)S(1)}, u32[]{:S(2)}, u32[]{:S(2)}) collective-permute-start(bf16[192,512]{1,0:T(8,128)(2,1)S(1)} %shard_map.101), channel_id=1, source_target_pairs={{0,4},{1,5},{2,6},{3,7},{4,0},{5,1},{6,2},{7,3},{8,12},{9,13},{10,... | collective-permute-start | bytes 589832 | tf_op jit(solution)/shard_map/ppermute | solution.py:250
  38.7 5.3 %collective-permute-done.13.arrived = bf16[128,512]{1,0:T(8,128)(2,1)S(1)} collective-permute-done((bf16[128,512]{1,0:T(8,128)(2,1)S(1)}, bf16[128,512]{1,0:T(8,128)(2,1)S(1)}, u32[]{:S(2)}, u32[]{:S(2)}) %collective-permute-start.13) | collective-permute-done | bytes 131104 | tf_op jit(solution)/shard_map/ppermute | solution.py:250
  44.0 0.1 collective-permute-start.14
  44.1 0.0 copy-done.2
  44.1 0.7 %shard_map.99 = (f32[512,256]{1,0:T(8,128)S(1)}, f32[64,512]{1,0:T(8,128)S(1)}) custom-call(f32[256,256]{1,0:T(8,128)S(1)} %get-tuple-element.23.basis, f32[1,512,256]{2,1,0:T(8,128)S(1)} %copy-done.2), custom_call_target="tpu_custom_call" | custom-call | flops 201326592 | bytes 1048576 | tf_op jit(solution)/shard_map/pallas_call | solution.py:310
  44.7 5.8 %collective-permute-done.14.late = bf16[64,512]{1,0:T(8,128)(2,1)S(1)} collective-permute-done((bf16[64,512]{1,0:T(8,128)(2,1)S(1)}, bf16[64,512]{1,0:T(8,128)(2,1)S(1)}, u32[]{:S(2)}, u32[]{:S(2)}) %collective-permute-start.14) | collective-permute-done | bytes 65568 | tf_op jit(solution)/shard_map/ppermute | solution.py:250
  50.5 1.2 %collective-permute-start.15 = (bf16[64,512]{1,0:T(8,128)(2,1)S(1)}, bf16[64,512]{1,0:T(8,128)(2,1)S(1)}, u32[]{:S(2)}, u32[]{:S(2)}) collective-permute-start(bf16[64,512]{1,0:T(8,128)(2,1)S(1)} %shard_map.103.refs_0_), channel_id=1, source_target_pairs={{0,8},{8,0},{16,24},{24,16},{1,9},{9,1},{17,25},{25,17},{2,10},{10... | collective-permute-start | bytes 196616 | tf_op jit(solution)/shard_map/ppermute | solution.py:250
  51.8 0.0 collective-permute-done.3.theirs
  51.8 0.8 %collective-permute-start.16 = (bf16[64,512]{1,0:T(8,128)(2,1)S(1)}, bf16[64,512]{1,0:T(8,128)(2,1)S(1)}, u32[]{:S(2)}, u32[]{:S(2)}) collective-permute-start(bf16[64,512]{1,0:T(8,128)(2,1)S(1)} %shard_map.103.refs_0_), channel_id=1, source_target_pairs={{0,16},{8,24},{16,0},{24,8},{1,17},{9,25},{17,1},{25,9},{2,18},{10... | collective-permute-start | bytes 196616 | tf_op jit(solution)/shard_map/ppermute | solution.py:250
  52.6 0.0 collective-permute-done.7.theirs
  52.6 1.5 %collective-permute-start.17 = (bf16[64,512]{1,0:T(8,128)(2,1)S(1)}, bf16[64,512]{1,0:T(8,128)(2,1)S(1)}, u32[]{:S(2)}, u32[]{:S(2)}) collective-permute-start(bf16[64,512]{1,0:T(8,128)(2,1)S(1)} %shard_map.103.refs_0_), channel_id=1, source_target_pairs={{0,24},{8,16},{16,8},{24,0},{1,25},{9,17},{17,9},{25,1},{2,26},{10... | collective-permute-start | bytes 196616 | tf_op jit(solution)/shard_map/ppermute | solution.py:250
  54.1 0.0 copy-done.1
  54.1 1.2 %shard_map.96._ = bf16[192,4096]{1,0:T(8,128)(2,1)} custom-call(bf16[192,256]{1,0:T(8,128)(2,1)S(1)} %copy-done.1, bf16[896,256]{1,0:T(8,128)(2,1)S(1)} %shard_map.95.mine, bf16[896,256]{1,0:T(8,128)(2,1)S(1)} %collective-permute-done.3.theirs), custom_call_target="tpu_custom_call" | custom-call | flops 201326592 | bytes 786432 | tf_op jit(solution)/shard_map/pallas_call | solution.py:340
  55.3 0.0 copy-start
  55.3 1.4 %shard_map.98 = bf16[192,4096]{1,0:T(8,128)(2,1)} custom-call(bf16[192,4096]{1,0:T(8,128)(2,1)} %shard_map.96._, bf16[192,256]{1,0:T(8,128)(2,1)S(1)} %copy-done.1, bf16[1152,256]{1,0:T(8,128)(2,1)S(1)} %shard_map.97.mine, bf16[1152,256]{1,0:T(8,128)(2,1)S(1)} %collective-permute-done.7.theirs), custom_call_target="tpu_custom_call", output_to_operand_aliasing={{}: (0, {})} | custom-call | flops 201326592 | bytes 786432 | tf_op jit(solution)/shard_map/pallas_call | solution.py:350
  56.7 0.0 collective-permute-done.10.near
  56.7 0.0 collective-permute-done.15.refs_1_
  56.7 0.0 collective-permute-done.16.refs_2_
  56.7 1.1 %collective-permute-done.17.refs_3_ = bf16[64,512]{1,0:T(8,128)(2,1)S(1)} collective-permute-done((bf16[64,512]{1,0:T(8,128)(2,1)S(1)}, bf16[64,512]{1,0:T(8,128)(2,1)S(1)}, u32[]{:S(2)}, u32[]{:S(2)}) %collective-permute-start.17) | collective-permute-done | bytes 65568 | tf_op jit(solution)/shard_map/ppermute | solution.py:250
  57.8 0.0 collective-permute-done.12.late
  57.8 0.0 copy-done
  57.8 1.5 %shard_map.104 = (f32[1,512,256]{2,1,0:T(8,128)}, f32[512,256]{1,0:T(8,128)}, f32[512,256]{1,0:T(8,128)}) custom-call(f32[256,256]{1,0:T(8,128)S(1)} %get-tuple-element.23.basis, f32[512,256]{1,0:T(8,128)S(1)} %get-tuple-element.24.kept, f32[192,512]{1,0:T(8,128)S(1)} %get-tuple-element.27.own, bf16[192,512]{1,0:T(8,128)(2,1)S(1)} %collective-permute-done.10.near, ...), custom_call_target="tpu_custom_call" | custom-call | flops 67108864 | bytes 3670016 | tf_op jit(solution)/shard_map/pallas_call | solution.py:320
  (6 shorter events, 0.2 us)
Async XLA Ops:
  0.6 27.0 %collective-permute-start.9 = (bf16[192,4096]{1,0:T(8,128)(2,1)}, bf16[192,4096]{1,0:T(8,128)(2,1)S(1)}, u32[]{:S(2)}, u32[]{:S(2)}) collective-permute-start(bf16[192,4096]{1,0:T(8,128)(2,1)} %tokens.1), channel_id=1, source_target_pairs={{0,1},{1,0},{2,3},{3,2},{4,5},{5,4},{6,7},{7,6},{8,9},{9,8},{10,11... | collective-permute-start | bytes 4718600 | tf_op jit(solution)/shard_map/ppermute | solution.py:250
  2.7 5.4 %collective-permute-start = (bf16[128,256]{1,0:T(8,128)(2,1)S(1)}, bf16[128,256]{1,0:T(8,128)(2,1)S(1)}, u32[]{:S(2)}, u32[]{:S(2)}) collective-permute-start(bf16[128,256]{1,0:T(8,128)(2,1)S(1)} %get-tuple-element.22), channel_id=1, source_target_pairs={{0,2},{1,3},{2,0},{3,1},{4,6},{5,7},{6,4},{7,5},{8,10},{9,11},{10,... | collective-permute-start | bytes 196616 | tf_op jit(solution)/shard_map/ppermute | solution.py:250
  5.4 7.0 %collective-permute-start.1 = (bf16[128,256]{1,0:T(8,128)(2,1)S(1)}, bf16[128,256]{1,0:T(8,128)(2,1)S(1)}, u32[]{:S(2)}, u32[]{:S(2)}) collective-permute-start(bf16[128,256]{1,0:T(8,128)(2,1)S(1)} %get-tuple-element.22), channel_id=1, source_target_pairs={{0,4},{1,5},{2,6},{3,7},{4,0},{5,1},{6,2},{7,3},{8,12},{9,13},{10,... | collective-permute-start | bytes 196616 | tf_op jit(solution)/shard_map/ppermute | solution.py:250
  8.0 6.1 %collective-permute-start.2 = (bf16[128,256]{1,0:T(8,128)(2,1)S(1)}, bf16[128,256]{1,0:T(8,128)(2,1)S(1)}, u32[]{:S(2)}, u32[]{:S(2)}) collective-permute-start(bf16[128,256]{1,0:T(8,128)(2,1)S(1)} %get-tuple-element.22), channel_id=1, source_target_pairs={{0,6},{1,7},{2,4},{3,5},{4,2},{5,3},{6,0},{7,1},{8,14},{9,15},{10,... | collective-permute-start | bytes 196616 | tf_op jit(solution)/shard_map/ppermute | solution.py:250
  14.0 7.6 %collective-permute-start.4 = (bf16[384,256]{1,0:T(8,128)(2,1)S(1)}, bf16[384,256]{1,0:T(8,128)(2,1)S(1)}, u32[]{:S(2)}, u32[]{:S(2)}) collective-permute-start(bf16[384,256]{1,0:T(8,128)(2,1)S(1)} %shard_map.94.refs_1_), channel_id=1, source_target_pairs={{0,8},{8,0},{16,24},{24,16},{1,9},{9,1},{17,25},{25,17},{2,10},{10... | collective-permute-start | bytes 589832 | tf_op jit(solution)/shard_map/ppermute | solution.py:250
  15.6 9.8 %collective-permute-start.5 = (bf16[384,256]{1,0:T(8,128)(2,1)S(1)}, bf16[384,256]{1,0:T(8,128)(2,1)S(1)}, u32[]{:S(2)}, u32[]{:S(2)}) collective-permute-start(bf16[384,256]{1,0:T(8,128)(2,1)S(1)} %shard_map.94.refs_1_), channel_id=1, source_target_pairs={{0,16},{8,24},{16,0},{24,8},{1,17},{9,25},{17,1},{25,9},{2,18},{10... | collective-permute-start | bytes 589832 | tf_op jit(solution)/shard_map/ppermute | solution.py:250
  17.1 8.3 %collective-permute-start.6 = (bf16[384,256]{1,0:T(8,128)(2,1)S(1)}, bf16[384,256]{1,0:T(8,128)(2,1)S(1)}, u32[]{:S(2)}, u32[]{:S(2)}) collective-permute-start(bf16[384,256]{1,0:T(8,128)(2,1)S(1)} %shard_map.94.refs_1_), channel_id=1, source_target_pairs={{0,24},{8,16},{16,8},{24,0},{1,25},{9,17},{17,9},{25,1},{2,26},{10... | collective-permute-start | bytes 589832 | tf_op jit(solution)/shard_map/ppermute | solution.py:250
  25.4 27.2 %collective-permute-start.7 = (bf16[1152,256]{1,0:T(8,128)(2,1)S(1)}, bf16[1152,256]{1,0:T(8,128)(2,1)S(1)}, u32[]{:S(2)}, u32[]{:S(2)}) collective-permute-start(bf16[1152,256]{1,0:T(8,128)(2,1)S(1)} %shard_map.97.mine), channel_id=1, source_target_pairs={{0,1},{1,0},{2,3},{3,2},{4,5},{5,4},{6,7},{7,6},{8,9},{9,8},{10,11... | collective-permute-start | bytes 1769480 | tf_op jit(solution)/shard_map/ppermute | solution.py:250
  25.5 2.2 %collective-permute-start.8 = (bf16[256,192]{1,0:T(8,128)(2,1)S(1)}, bf16[256,192]{1,0:T(8,128)(2,1)S(1)}, u32[]{:S(2)}, u32[]{:S(2)}) collective-permute-start(bf16[256,192]{1,0:T(8,128)(2,1)S(1)} %get-tuple-element.25.mine), channel_id=1, source_target_pairs={{0,1},{1,0},{2,3},{3,2},{4,5},{5,4},{6,7},{7,6},{8,9},{9,8},{10,11... | collective-permute-start | bytes 294920 | tf_op jit(solution)/shard_map/ppermute | solution.py:250
  26.0 25.8 %collective-permute-start.3 = (bf16[896,256]{1,0:T(8,128)(2,1)S(1)}, bf16[896,256]{1,0:T(8,128)(2,1)S(1)}, u32[]{:S(2)}, u32[]{:S(2)}) collective-permute-start(bf16[896,256]{1,0:T(8,128)(2,1)S(1)} %shard_map.95.mine), channel_id=1, source_target_pairs={{0,1},{1,0},{2,3},{3,2},{4,5},{5,4},{6,7},{7,6},{8,9},{9,8},{10,11... | collective-permute-start | bytes 1376264 | tf_op jit(solution)/shard_map/ppermute | solution.py:250
  27.7 16.4 %copy-start.2 = (f32[1,512,256]{2,1,0:T(8,128)S(1)}, f32[1,512,256]{2,1,0:T(8,128)}, u32[]{:S(2)}) copy-start(f32[1,512,256]{2,1,0:T(8,128)} %momentum.1) | copy-start | bytes 1572868
  28.4 25.7 %copy-start.1 = (bf16[192,256]{1,0:T(8,128)(2,1)S(1)}, bf16[192,256]{1,0:T(8,128)(2,1)}, u32[]{:S(2)}) copy-start(bf16[192,256]{1,0:T(8,128)(2,1)} %cot.5) | copy-start | bytes 294916
  28.4 7.8 %collective-permute-start.11 = (bf16[192,512]{1,0:T(8,128)(2,1)S(1)}, bf16[192,512]{1,0:T(8,128)(2,1)S(1)}, u32[]{:S(2)}, u32[]{:S(2)}) collective-permute-start(bf16[192,512]{1,0:T(8,128)(2,1)S(1)} %get-tuple-element.30), channel_id=1, source_target_pairs={{0,2},{1,3},{2,0},{3,1},{4,6},{5,7},{6,4},{7,5},{8,10},{9,11},{10,... | collective-permute-start | bytes 589832 | tf_op jit(solution)/shard_map/ppermute | solution.py:250
  30.4 13.6 %collective-permute-start.13 = (bf16[128,512]{1,0:T(8,128)(2,1)S(1)}, bf16[128,512]{1,0:T(8,128)(2,1)S(1)}, u32[]{:S(2)}, u32[]{:S(2)}) collective-permute-start(bf16[128,512]{1,0:T(8,128)(2,1)S(1)} %get-tuple-element.33), channel_id=1, source_target_pairs={{0,2},{1,3},{2,0},{3,1},{4,6},{5,7},{6,4},{7,5},{8,10},{9,11},{10,... | collective-permute-start | bytes 393224 | tf_op jit(solution)/shard_map/ppermute | solution.py:250
  30.5 26.2 %collective-permute-start.10 = (bf16[192,512]{1,0:T(8,128)(2,1)S(1)}, bf16[192,512]{1,0:T(8,128)(2,1)S(1)}, u32[]{:S(2)}, u32[]{:S(2)}) collective-permute-start(bf16[192,512]{1,0:T(8,128)(2,1)S(1)} %get-tuple-element.28), channel_id=1, source_target_pairs={{0,2},{1,3},{2,0},{3,1},{4,6},{5,7},{6,4},{7,5},{8,10},{9,11},{10,... | collective-permute-start | bytes 589832 | tf_op jit(solution)/shard_map/ppermute | solution.py:250
  36.3 21.5 %collective-permute-start.12 = (bf16[192,512]{1,0:T(8,128)(2,1)S(1)}, bf16[192,512]{1,0:T(8,128)(2,1)S(1)}, u32[]{:S(2)}, u32[]{:S(2)}) collective-permute-start(bf16[192,512]{1,0:T(8,128)(2,1)S(1)} %shard_map.101), channel_id=1, source_target_pairs={{0,4},{1,5},{2,6},{3,7},{4,0},{5,1},{6,2},{7,3},{8,12},{9,13},{10,... | collective-permute-start | bytes 589832 | tf_op jit(solution)/shard_map/ppermute | solution.py:250
  44.0 6.5 %collective-permute-start.14 = (bf16[64,512]{1,0:T(8,128)(2,1)S(1)}, bf16[64,512]{1,0:T(8,128)(2,1)S(1)}, u32[]{:S(2)}, u32[]{:S(2)}) collective-permute-start(bf16[64,512]{1,0:T(8,128)(2,1)S(1)} %shard_map.102), channel_id=1, source_target_pairs={{0,4},{1,5},{2,6},{3,7},{4,0},{5,1},{6,2},{7,3},{8,12},{9,13},{10,... | collective-permute-start | bytes 196616 | tf_op jit(solution)/shard_map/ppermute | solution.py:250
  50.5 6.1 %collective-permute-start.15 = (bf16[64,512]{1,0:T(8,128)(2,1)S(1)}, bf16[64,512]{1,0:T(8,128)(2,1)S(1)}, u32[]{:S(2)}, u32[]{:S(2)}) collective-permute-start(bf16[64,512]{1,0:T(8,128)(2,1)S(1)} %shard_map.103.refs_0_), channel_id=1, source_target_pairs={{0,8},{8,0},{16,24},{24,16},{1,9},{9,1},{17,25},{25,17},{2,10},{10... | collective-permute-start | bytes 196616 | tf_op jit(solution)/shard_map/ppermute | solution.py:250
  51.8 4.9 %collective-permute-start.16 = (bf16[64,512]{1,0:T(8,128)(2,1)S(1)}, bf16[64,512]{1,0:T(8,128)(2,1)S(1)}, u32[]{:S(2)}, u32[]{:S(2)}) collective-permute-start(bf16[64,512]{1,0:T(8,128)(2,1)S(1)} %shard_map.103.refs_0_), channel_id=1, source_target_pairs={{0,16},{8,24},{16,0},{24,8},{1,17},{9,25},{17,1},{25,9},{2,18},{10... | collective-permute-start | bytes 196616 | tf_op jit(solution)/shard_map/ppermute | solution.py:250
  52.6 5.2 %collective-permute-start.17 = (bf16[64,512]{1,0:T(8,128)(2,1)S(1)}, bf16[64,512]{1,0:T(8,128)(2,1)S(1)}, u32[]{:S(2)}, u32[]{:S(2)}) collective-permute-start(bf16[64,512]{1,0:T(8,128)(2,1)S(1)} %shard_map.103.refs_0_), channel_id=1, source_target_pairs={{0,24},{8,16},{16,8},{24,0},{1,25},{9,17},{17,9},{25,1},{2,26},{10... | collective-permute-start | bytes 196616 | tf_op jit(solution)/shard_map/ppermute | solution.py:250
  55.3 2.5 %copy-start = (f32[512,256]{1,0:T(8,128)S(1)}, f32[512,256]{1,0:T(8,128)}, u32[]{:S(2)}) copy-start(f32[512,256]{1,0:T(8,128)} %weight.3) | copy-start | bytes 1572868
